TPU v7x, 32 devices: a whole 2x2x4 slice. The times are simulated.
32 devices in a mesh: expert: 16 (over z, y, x), tok: 2 (over core).
Axes of the slice: x: 2, y: 2, z: 4, core: 2. Of those that a mesh axis runs over, the one named last changes fastest.
Arguments:
- tokens: bfloat16 [2048, 3584], P(('expert', 'tok')), may hold values from -6 to 6
- routes: int32 [2048, 8], P(('expert', 'tok')), may hold values from 0 to 15, all different within a row; in each aligned block of 64 rows (0 to 63, 64 to 127, ...) at most 36 rows name the same one
- gates: float32 [2048, 8], P(('expert', 'tok')), may hold values from 0.05 to 1
- upstream: bfloat16 [2048, 3584], P(('expert', 'tok')), may hold values from -6 to 6
- w_up: bfloat16 [16, 3584, 1024], P('expert', None, 'tok'), may hold values from -0.09375 to 0.09375
- w_down: bfloat16 [16, 1024, 3584], P('expert', 'tok'), may hold values from -0.1875 to 0.1875
Outputs:
- mixed: bfloat16 [2048, 3584], P(('expert', 'tok'))
- d_tokens: bfloat16 [2048, 3584], P(('expert', 'tok'))
- d_gates: float32 [2048, 8], P(('expert', 'tok'))
- grad_up: bfloat16 [16, 3584, 1024], P('expert', None, 'tok')
- grad_down: bfloat16 [16, 1024, 3584], P('expert', 'tok')
Inputs may be any that keep to these rules, and one draw needn't show every extreme that they name: `routes`: each token names 8 different experts. At most 36 of the 64 tokens of one device name the same expert, and in every draw the tokens of some device name some expert exactly 36 times.
All inputs are finite; a program needn't handle non-finite values.
Results may differ from a plain program's by a relative error of at most 0.0065.
Values may be sent and summed in bfloat16 or wider, within the bound.
A program may use at most 192 MiB of HBM per device.

v0:
```python
import jax
import jax.numpy as jnp
from jax import lax
from jax.sharding import PartitionSpec as P

GELU_C = 0.7978845608028654
GELU_A = 0.044715


def gelu_value(hidden):
    inner_arg = GELU_C * (hidden + GELU_A * hidden * hidden * hidden)
    return 0.5 * hidden * (1.0 + jnp.tanh(inner_arg))


def gelu_slope(hidden):
    tangent = jnp.tanh(GELU_C * (hidden + GELU_A * hidden * hidden * hidden))
    return 0.5 * (1.0 + tangent) + 0.5 * hidden * (1.0 - tangent * tangent) * GELU_C * (
        1.0 + 3.0 * GELU_A * hidden * hidden
    )


def expert_rows(rows_x, rows_grad, up_local, down_local):
    hidden = jnp.dot(rows_x, up_local, preferred_element_type=jnp.float32)
    active = gelu_value(hidden).astype(jnp.bfloat16)
    out_part = jnp.dot(active, down_local, preferred_element_type=jnp.float32)
    d_active = lax.dot_general(
        rows_grad, down_local, (((1,), (1,)), ((), ())), preferred_element_type=jnp.float32
    )
    d_hidden = (d_active * gelu_slope(hidden)).astype(jnp.bfloat16)
    dx_part = lax.dot_general(
        d_hidden, up_local, (((1,), (1,)), ((), ())), preferred_element_type=jnp.float32
    )
    grad_down = lax.dot_general(
        active, rows_grad, (((0,), (0,)), ((), ())), preferred_element_type=jnp.float32
    )
    grad_up = lax.dot_general(
        rows_x, d_hidden, (((0,), (0,)), ((), ())), preferred_element_type=jnp.float32
    )
    return (out_part, dx_part, grad_up, grad_down)


def routed_shards(tokens, routes, gates, upstream, w_up, w_down):
    tok_rows, feature_width = tokens.shape
    top_count = routes.shape[1]
    owners = lax.axis_size("expert")
    pair_count = lax.axis_size("tok")
    capacity = tok_rows * top_count // owners + max(1, tok_rows * top_count // (8 * owners))
    assigned = routes.reshape(-1)
    labels = jnp.arange(owners, dtype=jnp.int32)
    onehot = (assigned[:, None] == labels[None, :]).astype(jnp.int32)
    earlier = jnp.cumsum(onehot, axis=0) - onehot
    slot_rank = jnp.sum(earlier * onehot, axis=1)
    slot_of = assigned * capacity + slot_rank
    slot_ids = jnp.arange(owners * capacity, dtype=jnp.int32)
    matches = (slot_of[None, :] == slot_ids[:, None]).astype(jnp.int32)
    filled = jnp.sum(matches, axis=1) > 0
    source = jnp.sum(matches * jnp.arange(assigned.shape[0], dtype=jnp.int32)[None, :], axis=1)
    token_ids = source // top_count
    send_x = jnp.where(filled[:, None], tokens[token_ids], jnp.zeros((), jnp.bfloat16))
    gate_rows = jnp.where(filled, gates.reshape(-1)[source], jnp.zeros((), jnp.float32))
    send_grad = (gate_rows[:, None] * upstream[token_ids].astype(jnp.float32)).astype(jnp.bfloat16)
    send_x = send_x.reshape(owners, capacity, feature_width)
    send_grad = send_grad.reshape(owners, capacity, feature_width)
    recv_x, recv_grad = (
        lax.all_to_all(send_x, "expert", split_axis=0, concat_axis=0, tiled=True),
        lax.all_to_all(send_grad, "expert", split_axis=0, concat_axis=0, tiled=True),
    )
    both_x, both_grad = (
        lax.all_gather(recv_x[None], "tok", axis=0, tiled=True),
        lax.all_gather(recv_grad[None], "tok", axis=0, tiled=True),
    )
    rows_x = both_x.reshape(-1, feature_width)
    rows_grad = both_grad.reshape(-1, feature_width)
    out_part, dx_part, grad_up, grad_down = expert_rows(rows_x, rows_grad, w_up[0], w_down[0])
    shaped_out = out_part.reshape(pair_count, owners, capacity, feature_width)
    shaped_dx = dx_part.reshape(pair_count, owners, capacity, feature_width)
    summed_out, summed_dx = (
        lax.psum_scatter(shaped_out, "tok", scatter_dimension=0, tiled=True),
        lax.psum_scatter(shaped_dx, "tok", scatter_dimension=0, tiled=True),
    )
    home_out, home_dx = (
        lax.all_to_all(
            summed_out[0].astype(jnp.bfloat16), "expert", split_axis=0, concat_axis=0, tiled=True
        ),
        lax.all_to_all(
            summed_dx[0].astype(jnp.bfloat16), "expert", split_axis=0, concat_axis=0, tiled=True
        ),
    )
    out_pairs = (
        home_out.reshape(owners * capacity, feature_width)[slot_of]
        .reshape(tok_rows, top_count, feature_width)
        .astype(jnp.float32)
    )
    dx_pairs = (
        home_dx.reshape(owners * capacity, feature_width)[slot_of]
        .reshape(tok_rows, top_count, feature_width)
        .astype(jnp.float32)
    )
    mixed_out = jnp.sum(gates[:, :, None] * out_pairs, axis=1).astype(jnp.bfloat16)
    d_gates = jnp.sum(upstream.astype(jnp.float32)[:, None, :] * out_pairs, axis=2)
    d_tokens = jnp.sum(dx_pairs, axis=1).astype(jnp.bfloat16)
    return (
        mixed_out,
        d_tokens,
        d_gates,
        grad_up.astype(jnp.bfloat16)[None],
        grad_down.astype(jnp.bfloat16)[None],
    )


def swapped(array, bit):
    return lax.ppermute(array, "expert", tuple(((i, i ^ bit) for i in range(16))))


def shifted(array, step, senders):
    return lax.ppermute(
        array,
        "expert",
        tuple(((i, i + 4 * step) for z in senders for i in range(4 * z, 4 * z + 4))),
    )


def add_rows(first, *others):
    total = first.astype(jnp.float32)
    for other in others:
        total = total + other.astype(jnp.float32)
    return total.astype(jnp.bfloat16)


def gathered_slots(block, layer, first, second):
    up_one = shifted(block, 1, (0, 1, 2))
    down_one = shifted(block, -1, (3, 2, 1))
    up_two = shifted(up_one, 1, (1, 2))
    down_two = shifted(down_one, -1, (2, 1))
    up_three = shifted(up_two, 1, (2,))
    down_three = shifted(down_two, -1, (1,))
    low = layer < 2
    far = jnp.where(
        low, jnp.where(layer == 0, down_three, up_one), jnp.where(layer == 3, up_three, down_one)
    )
    columns = (block, jnp.where(low, down_one, up_one), jnp.where(low, down_two, up_two), far)
    slots = []
    for column in columns:
        pair = jnp.stack([column, swapped(column, first)])
        other = swapped(pair, second)
        if first == 1:
            slots.append(jnp.concatenate([pair[0], pair[1], other[0], other[1]], axis=0))
        else:
            slots.append(jnp.concatenate([pair[0], other[0], pair[1], other[1]], axis=0))
    return slots


def scattered_column(rows, tok_rows, first, second):
    blocks = [rows[i * tok_rows : (i + 1) * tok_rows].astype(jnp.bfloat16) for i in range(4)]
    kept, sent = ((0, 1), (2, 3)) if first == 2 else ((0, 2), (1, 3))
    came = swapped(jnp.stack([blocks[i] for i in sent]), first)
    near = add_rows(blocks[kept[0]], came[0])
    far = add_rows(blocks[kept[1]], came[1])
    return add_rows(near, swapped(far, second))


def scattered_layers(columns, layer):
    up = shifted(columns[3], 1, (0,))
    down = shifted(columns[3], -1, (3,))
    up = shifted(add_rows(columns[2], up), 1, (0, 1))
    down = shifted(add_rows(columns[2], down), -1, (3, 2))
    up = shifted(add_rows(jnp.where(layer == 2, columns[3], columns[1]), up), 1, (0, 1, 2))
    down = shifted(add_rows(jnp.where(layer == 1, columns[3], columns[1]), down), -1, (3, 2, 1))
    return add_rows(columns[0], up, down)


def transposed_dot(rows, weights):
    return lax.dot_general(
        rows, weights, (((1,), (1,)), ((), ())), preferred_element_type=jnp.float32
    )


def outer(rows, columns):
    return lax.dot_general(
        rows, columns, (((0,), (0,)), ((), ())), preferred_element_type=jnp.float32
    )


def dense_shards(tokens, routes, gates, upstream, w_up, w_down):
    tok_rows, width = tokens.shape
    owners = lax.axis_size("expert")
    half = w_up.shape[2]
    swap = ((0, 1), (1, 0))
    mine = lax.axis_index("expert")
    layer = mine // 4
    up_local, down_local = (w_up[0], w_down[0])
    named = routes[:, :, None] == jnp.arange(owners, dtype=jnp.int32)
    gate_of = jnp.sum(jnp.where(named, gates[:, :, None], 0.0), axis=1)
    gate_all = lax.all_gather(gate_of, "expert", axis=0, tiled=True).reshape(
        owners, tok_rows, owners
    )
    gate_mine = lax.dynamic_index_in_dim(gate_all, mine, axis=2, keepdims=False)
    layers = (
        layer,
        jnp.where(layer < 2, layer + 1, layer - 1),
        jnp.where(layer < 2, layer + 2, layer - 2),
        jnp.where(layer % 2 == 0, 3, 0),
    )
    sources = [jnp.stack([z * 4 + (mine % 4 ^ flip) for flip in range(4)]) for z in layers]
    slots_x = gathered_slots(tokens, layer, 1, 2)
    slots_u = gathered_slots(upstream, layer, 2, 1)
    up_full = jnp.concatenate([up_local, lax.ppermute(up_local, "tok", swap)], axis=1)
    down_full = jnp.concatenate([down_local, lax.ppermute(down_local, "tok", swap)], axis=0)
    gated, slopes, inners = ([None] * 4, [None] * 4, [None] * 4)
    mixed_columns, dx_columns = ([None] * 4, [None] * 4)
    for s in range(4):
        gate = gate_mine[sources[s]].reshape(-1)[:, None]
        hidden = jnp.dot(slots_x[s], up_full, preferred_element_type=jnp.float32)
        value = gelu_value(hidden)
        gated[s] = (gate * value).astype(jnp.bfloat16)
        back = transposed_dot(slots_u[s], down_full)
        inners[s] = jnp.sum(value * back, axis=1).reshape(4, tok_rows)
        slopes[s] = (gate * back * gelu_slope(hidden)).astype(jnp.bfloat16)
    for s in (3, 2, 1, 0):
        out_part = jnp.dot(gated[s], down_full, preferred_element_type=jnp.float32)
        mixed_columns[s] = scattered_column(out_part, tok_rows, 2, 1)
        dx_part = transposed_dot(slopes[s], up_full)
        dx_columns[s] = scattered_column(dx_part, tok_rows, 1, 2)
    mixed = scattered_layers(mixed_columns, layer)
    d_tokens = scattered_layers(dx_columns, layer)
    order = jnp.concatenate(sources)
    inner = jnp.zeros((owners, tok_rows), jnp.float32).at[order].set(jnp.concatenate(inners))
    inner_all = lax.all_gather(inner, "expert", axis=0, tiled=True).reshape(
        owners, owners, tok_rows
    )
    home = lax.dynamic_index_in_dim(inner_all, mine, axis=1, keepdims=False)
    d_gates = jnp.sum(jnp.where(named, home.T[:, None, :], 0.0), axis=2)
    all_x, all_u = (jnp.concatenate(slots_x), jnp.concatenate(slots_u))
    act, d_hidden = (jnp.concatenate(gated), jnp.concatenate(slopes))
    down_far = outer(act[:, half:], all_u).astype(jnp.bfloat16)
    up_far = outer(all_x, d_hidden[:, half:]).astype(jnp.bfloat16)
    down_near = outer(act[:, :half], all_u)
    up_near = outer(all_x, d_hidden[:, :half])
    grad_down = down_near + lax.ppermute(down_far, "tok", swap).astype(jnp.float32)
    grad_up = up_near + lax.ppermute(up_far, "tok", swap).astype(jnp.float32)
    return (
        mixed,
        d_tokens,
        d_gates,
        grad_up.astype(jnp.bfloat16)[None],
        grad_down.astype(jnp.bfloat16)[None],
    )


def shards(tokens, routes, gates, upstream, w_up, w_down):
    dense = lax.axis_size("expert") == 16 and lax.axis_size("tok") == 2
    body = dense_shards if dense else routed_shards
    return body(tokens, routes, gates, upstream, w_up, w_down)


def solution(mesh):
    return jax.shard_map(
        shards,
        mesh=mesh,
        in_specs=(
            P(("expert", "tok"), None),
            P(("expert", "tok"), None),
            P(("expert", "tok"), None),
            P(("expert", "tok"), None),
            P("expert", None, "tok"),
            P("expert", "tok", None),
        ),
        out_specs=(
            P(("expert", "tok"), None),
            P(("expert", "tok"), None),
            P(("expert", "tok"), None),
            P("expert", None, "tok"),
            P("expert", "tok", None),
        ),
        check_vma=False,
    )
```

profile of v0, /device:TPU:20, one launch (start us, length us, event | category | flops | bytes accessed | tf_op | source)
XLA Modules:
  0.0 542.9 jit_solution(3025906620837556485)
XLA Ops:
  0.6 2.5 collective-permute-start.6
  4.7 3.5 collective-permute-start.9
  8.2 2.3 collective-permute-start.34
  18.8 5.5 %collective-permute-done.30 = bf16[64,3584]{1,0:T(8,128)(2,1)S(1)} collective-permute-done((bf16[64,3584]{1,0:T(8,128)(2,1)}, bf16[64,3584]{1,0:T(8,128)(2,1)S(1)}, u32[]{:S(2)}, u32[]{:S(2)}) %collective-permute-start.30) | collective-permute-done | bytes 458784 | tf_op jit(solution)/shard_map/ppermute | solution.py:112
  24.3 3.5 collective-permute-start.37
  27.9 13.7 %collective-permute-done.1 = bf16[2,64,3584]{2,1,0:T(8,128)(2,1)S(1)} collective-permute-done((bf16[2,64,3584]{2,1,0:T(8,128)(2,1)S(1)}, bf16[2,64,3584]{2,1,0:T(8,128)(2,1)S(1)}, u32[]{:S(2)}, u32[]{:S(2)}) %collective-permute-start.1) | collective-permute-done | bytes 917536 | tf_op jit(solution)/shard_map/ppermute | solution.py:112
  43.8 17.9 %collective-permute-done.31 = bf16[2,64,3584]{2,1,0:T(8,128)(2,1)S(1)} collective-permute-done((bf16[2,64,3584]{2,1,0:T(8,128)(2,1)S(1)}, bf16[2,64,3584]{2,1,0:T(8,128)(2,1)S(1)}, u32[]{:S(2)}, u32[]{:S(2)}) %collective-permute-start.31) | collective-permute-done | bytes 917536 | tf_op jit(solution)/shard_map/ppermute | solution.py:112
  63.9 3.2 collective-permute-start.7
  71.0 9.9 %collective-permute-done.16 = bf16[64,3584]{1,0:T(8,128)(2,1)S(1)} collective-permute-done((bf16[64,3584]{1,0:T(8,128)(2,1)S(1)}, bf16[64,3584]{1,0:T(8,128)(2,1)S(1)}, u32[]{:S(2)}, u32[]{:S(2)}) %collective-permute-start.16) | collective-permute-done | bytes 458784 | tf_op jit(solution)/shard_map/ppermute | solution.py:112
  82.4 2.1 collective-permute-start.10
  84.6 17.6 %collective-permute-done.17 = bf16[2,64,3584]{2,1,0:T(8,128)(2,1)S(1)} collective-permute-done((bf16[2,64,3584]{2,1,0:T(8,128)(2,1)S(1)}, bf16[2,64,3584]{2,1,0:T(8,128)(2,1)S(1)}, u32[]{:S(2)}, u32[]{:S(2)}) %collective-permute-start.17) | collective-permute-done | bytes 917536 | tf_op jit(solution)/shard_map/ppermute | solution.py:112
  104.9 17.5 %collective-permute-done.45 = bf16[2,64,3584]{2,1,0:T(8,128)(2,1)S(1)} collective-permute-done((bf16[2,64,3584]{2,1,0:T(8,128)(2,1)S(1)}, bf16[2,64,3584]{2,1,0:T(8,128)(2,1)S(1)}, u32[]{:S(2)}, u32[]{:S(2)}) %collective-permute-start.45) | collective-permute-done | bytes 917536 | tf_op jit(solution)/shard_map/ppermute | solution.py:112
  122.4 2.8 collective-permute-start.35
  133.1 2.1 collective-permute-start.11
  135.2 4.6 collective-permute-done.38
  143.7 4.6 collective-permute-done.20
  150.6 6.1 %collective-permute-done.48 = bf16[64,3584]{1,0:T(8,128)(2,1)S(1)} collective-permute-done((bf16[64,3584]{1,0:T(8,128)(2,1)S(1)}, bf16[64,3584]{1,0:T(8,128)(2,1)S(1)}, u32[]{:S(2)}, u32[]{:S(2)}) %collective-permute-start.48) | collective-permute-done | bytes 458784 | tf_op jit(solution)/shard_map/ppermute | solution.py:112
  159.2 5.4 collective-permute-start.39
  164.6 2.1 fusion.2
  167.3 3.2 multiply_reduce_fusion.3
  170.4 3.0 fusion.18
  173.6 6.8 %multiply_reduce_fusion.2 = (f32[256]{0:T(256)S(1)}, f32[256,1024]{1,0:T(8,128)}) fusion(f32[256,1024]{1,0:T(8,128)} %fusion.18, bf16[512,3584]{1,0:T(8,128)(2,1)} %copy-done.39, bf16[512,3584]{1,0:T(8,128)(2,1)} %bitcast.290, bf16[64,3584]{1,0:T(8,128)(2,1)} %get-tuple-element.58, bf16[64,3584]{1,0:T(8,128)(2,1)S(1)} %collective-permute-done.44, ...), kind=kOutput, calls=%fused_computation.133 | convolution fusion | flops 1903689472 | bytes 11273216 | tf_op jit(solution)/shard_map/dot_general | solution.py:173
  183.1 2.4 constant_dynamic-update-slice_fusion.3
  186.5 11.9 %collective-permute-done.49 = bf16[2,64,3584]{2,1,0:T(8,128)(2,1)S(1)} collective-permute-done((bf16[2,64,3584]{2,1,0:T(8,128)(2,1)}, bf16[2,64,3584]{2,1,0:T(8,128)(2,1)S(1)}, u32[]{:S(2)}, u32[]{:S(2)}) %collective-permute-start.49) | collective-permute-done | bytes 917536 | tf_op jit(solution)/shard_map/ppermute | solution.py:112
  201.0 2.1 fusion.26
  205.0 3.2 multiply_reduce_fusion.1
  211.7 5.0 collective-permute-done.40
  220.1 6.6 %collective-permute-done.13 = bf16[2,64,3584]{2,1,0:T(8,128)(2,1)S(1)} collective-permute-done((bf16[2,64,3584]{2,1,0:T(8,128)(2,1)S(1)}, bf16[2,64,3584]{2,1,0:T(8,128)(2,1)S(1)}, u32[]{:S(2)}, u32[]{:S(2)}) %collective-permute-start.13) | collective-permute-done | bytes 917536 | tf_op jit(solution)/shard_map/ppermute | solution.py:112
  226.8 3.9 collective-permute-done.41
  230.8 3.2 fusion.10
  234.1 3.6 multiply_reduce_fusion
  238.4 33.8 %all_gather.7 = f32[256,64]{1,0:T(8,128)S(1)} all-gather(f32[16,64]{1,0:T(8,128)S(1)} %scatter_custom_fusion), channel_id=1, replica_groups=mesh['expert'=16,'tok'=2] {'expert'}, dimensions={0}, use_global_device_ids=true | all-gather | bytes 69632 | tf_op jit(solution)/shard_map/all_gather | solution.py:228
  272.8 33.2 %all-gather = f32[16,64,16]{1,2,0:T(8,128)S(1)} all-gather(f32[1,64,16]{1,2,0:T(8,128)S(1)} %bitcast.279), channel_id=1, replica_groups=mesh['expert'=16,'tok'=2] {'expert'}, dimensions={0}, use_global_device_ids=true | all-gather | bytes 69632 | tf_op jit(solution)/shard_map/all_gather | solution.py:194
  308.6 2.4 fusion.78
  310.9 5.3 convolution_convert_fusion.5
  316.4 2.5 collective-permute-start.32
  319.8 4.2 convolution_convert_fusion.3
  328.6 5.3 convolution_convert_fusion.4
  334.0 5.3 convolution_convert_fusion.2
  341.7 4.3 convolution_convert_fusion.9
  346.2 4.1 convolution_convert_fusion.7
  350.6 5.2 convolution_convert_fusion.8
  355.9 5.2 convolution_convert_fusion.6
  364.1 8.6 %convolution_convert_fusion = bf16[512,3584]{1,0:T(8,128)(2,1)} fusion(bf16[1024,3584]{1,0:T(8,128)(2,1)} %constant_dynamic-update-slice_fusion.16, bf16[1024,1024]{1,0:T(8,128)(2,1)S(1)} %pad_maximum_fusion.3), kind=kOutput, calls=%fused_computation.9 | convolution fusion | flops 3759931392 | bytes 12058624 | tf_op jit(solution)/shard_map/dot_general | solution.py:179
  374.2 8.6 %convolution_convert_fusion.1 = bf16[3584,512]{1,0:T(8,128)(2,1)} fusion(bf16[1024,3584]{1,0:T(8,128)(2,1)} %constant_dynamic-update-slice_fusion, bf16[1024,1024]{1,0:T(8,128)(2,1)S(1)} %pad_maximum_fusion.2), kind=kOutput, calls=%fused_computation.10 | convolution fusion | flops 3759931392 | bytes 12058624 | tf_op jit(solution)/shard_map/dot_general | solution.py:179
  392.3 10.4 %collective-permute-done.18 = bf16[2,64,3584]{2,1,0:T(8,128)(2,1)S(1)} collective-permute-done((bf16[2,64,3584]{2,1,0:T(8,128)(2,1)S(1)}, bf16[2,64,3584]{2,1,0:T(8,128)(2,1)S(1)}, u32[]{:S(2)}, u32[]{:S(2)}) %collective-permute-start.18) | collective-permute-done | bytes 917536 | tf_op jit(solution)/shard_map/ppermute | solution.py:112
  402.9 25.5 %collective-permute-done.14 = bf16[2,64,3584]{2,1,0:T(8,128)(2,1)S(1)} collective-permute-done((bf16[2,64,3584]{2,1,0:T(8,128)(2,1)S(1)}, bf16[2,64,3584]{2,1,0:T(8,128)(2,1)S(1)}, u32[]{:S(2)}, u32[]{:S(2)}) %collective-permute-start.14) | collective-permute-done | bytes 917536 | tf_op jit(solution)/shard_map/ppermute | solution.py:112
  429.2 12.3 %collective-permute-done.43 = bf16[64,3584]{1,0:T(8,128)(2,1)S(1)} collective-permute-done((bf16[64,3584]{1,0:T(8,128)(2,1)S(1)}, bf16[64,3584]{1,0:T(8,128)(2,1)S(1)}, u32[]{:S(2)}, u32[]{:S(2)}) %collective-permute-start.43) | collective-permute-done | bytes 458784 | tf_op jit(solution)/shard_map/ppermute | solution.py:112
  445.5 17.4 %collective-permute-done.55 = bf16[64,3584]{1,0:T(8,128)(2,1)S(1)} collective-permute-done((bf16[64,3584]{1,0:T(8,128)(2,1)S(1)}, bf16[64,3584]{1,0:T(8,128)(2,1)S(1)}, u32[]{:S(2)}, u32[]{:S(2)}) %collective-permute-start.55) | collective-permute-done | bytes 458784 | tf_op jit(solution)/shard_map/ppermute | solution.py:116
  465.3 12.5 %collective-permute-done.27 = bf16[64,3584]{1,0:T(8,128)(2,1)S(1)} collective-permute-done((bf16[64,3584]{1,0:T(8,128)(2,1)S(1)}, bf16[64,3584]{1,0:T(8,128)(2,1)S(1)}, u32[]{:S(2)}, u32[]{:S(2)}) %collective-permute-start.27) | collective-permute-done | bytes 458784 | tf_op jit(solution)/shard_map/ppermute | solution.py:116
  479.1 4.6 collective-permute-start.56
  484.5 3.7 collective-permute-done.53
  489.5 2.4 collective-permute-done.56
  491.9 2.2 collective-permute-start.28
  495.6 2.9 collective-permute-done.25
  502.3 2.2 collective-permute-start.57
  505.5 3.5 collective-permute-done.54
  512.7 2.2 collective-permute-start.29
  514.8 2.1 add_convert_fusion.2
  516.9 2.4 collective-permute-done.26
  519.3 3.7 collective-permute-done.29
  523.0 2.1 add_convert_fusion.9
  525.1 8.9 %fusion = bf16[1,3584,512]{2,1,0:T(8,128)(2,1)} fusion(bf16[3584,512]{1,0:T(8,128)(2,1)S(1)} %collective-permute-done.58, bf16[1024,3584]{1,0:T(8,128)(2,1)} %constant_dynamic-update-slice_fusion, bf16[1024,1024]{1,0:T(8,128)(2,1)S(1)} %pad_maximum_fusion.2), kind=kOutput, calls=%fused_computation.11 | convolution fusion | flops 3763601408 | bytes 15728640 | tf_op jit(solution)/shard_map/dot_general | solution.py:179
  534.0 8.7 %fusion.1 = bf16[1,512,3584]{2,1,0:T(8,128)(2,1)} fusion(bf16[512,3584]{1,0:T(8,128)(2,1)S(1)} %collective-permute-done.59, bf16[1024,3584]{1,0:T(8,128)(2,1)} %constant_dynamic-update-slice_fusion.16, bf16[1024,1024]{1,0:T(8,128)(2,1)S(1)} %pad_maximum_fusion.3), kind=kOutput, calls=%fused_computation.12 | convolution fusion | flops 3763601408 | bytes 15728640 | tf_op jit(solution)/shard_map/dot_general | solution.py:179
  (280 shorter events, 101.6 us)
Async XLA Ops:
  0.6 62.7 %collective-permute-start.6 = (bf16[64,3584]{1,0:T(8,128)(2,1)}, bf16[64,3584]{1,0:T(8,128)(2,1)S(1)}, u32[]{:S(2)}, u32[]{:S(2)}) collective-permute-start(bf16[64,3584]{1,0:T(8,128)(2,1)} %param.6), channel_id=1, source_target_pairs={{24,16},{26,18},{28,20},{30,22},{16,8},{18,10},{20,12},{22,14},{8,... | collective-permute-start | bytes 1376264 | tf_op jit(solution)/shard_map/ppermute | solution.py:116
  3.1 12.3 %collective-permute-start = (bf16[64,3584]{1,0:T(8,128)(2,1)}, bf16[64,3584]{1,0:T(8,128)(2,1)S(1)}, u32[]{:S(2)}, u32[]{:S(2)}) collective-permute-start(bf16[64,3584]{1,0:T(8,128)(2,1)} %param.6), channel_id=1, source_target_pairs={{0,2},{2,0},{4,6},{6,4},{8,10},{10,8},{12,14},{14,12},{16,18},{18,... | collective-permute-start | bytes 1376264 | tf_op jit(solution)/shard_map/ppermute | solution.py:112
  4.7 59.2 %collective-permute-start.9 = (bf16[64,3584]{1,0:T(8,128)(2,1)}, bf16[64,3584]{1,0:T(8,128)(2,1)S(1)}, u32[]{:S(2)}, u32[]{:S(2)}) collective-permute-start(bf16[64,3584]{1,0:T(8,128)(2,1)} %param.6), channel_id=1, source_target_pairs={{0,8},{2,10},{4,12},{6,14},{8,16},{10,18},{12,20},{14,22},{16,24},... | collective-permute-start | bytes 1376264 | tf_op jit(solution)/shard_map/ppermute | solution.py:116
  8.2 60.5 %collective-permute-start.34 = (bf16[64,3584]{1,0:T(8,128)(2,1)}, bf16[64,3584]{1,0:T(8,128)(2,1)S(1)}, u32[]{:S(2)}, u32[]{:S(2)}) collective-permute-start(bf16[64,3584]{1,0:T(8,128)(2,1)} %param.9), channel_id=1, source_target_pairs={{24,16},{26,18},{28,20},{30,22},{16,8},{18,10},{20,12},{22,14},{8,... | collective-permute-start | bytes 1376264 | tf_op jit(solution)/shard_map/ppermute | solution.py:116
  10.5 13.7 %collective-permute-start.30 = (bf16[64,3584]{1,0:T(8,128)(2,1)}, bf16[64,3584]{1,0:T(8,128)(2,1)S(1)}, u32[]{:S(2)}, u32[]{:S(2)}) collective-permute-start(bf16[64,3584]{1,0:T(8,128)(2,1)} %param.9), channel_id=1, source_target_pairs={{0,4},{2,6},{4,0},{6,2},{8,12},{10,14},{12,8},{14,10},{16,20},{18,... | collective-permute-start | bytes 1376264 | tf_op jit(solution)/shard_map/ppermute | solution.py:112
  13.3 48.4 %copy-start.31 = (bf16[1,3584,512]{2,1,0:T(8,128)(2,1)S(1)}, bf16[1,3584,512]{2,1,0:T(8,128)(2,1)}, u32[]{:S(2)}) copy-start(bf16[1,3584,512]{2,1,0:T(8,128)(2,1)} %param.10) | copy-start | bytes 11010052
  16.5 25.1 %collective-permute-start.1 = (bf16[2,64,3584]{2,1,0:T(8,128)(2,1)S(1)}, bf16[2,64,3584]{2,1,0:T(8,128)(2,1)S(1)}, u32[]{:S(2)}, u32[]{:S(2)}) collective-permute-start(bf16[2,64,3584]{2,1,0:T(8,128)(2,1)S(1)} %pad_maximum_fusion.4), channel_id=1, source_target_pairs={{0,4},{2,6},{4,0},{6,2},{8,12},{10,14},{12,8},{14,10},{16,20},{18,... | collective-permute-start | bytes 2752520 | tf_op jit(solution)/shard_map/ppermute | solution.py:112
  24.3 45.0 %collective-permute-start.37 = (bf16[64,3584]{1,0:T(8,128)(2,1)S(1)}, bf16[64,3584]{1,0:T(8,128)(2,1)S(1)}, u32[]{:S(2)}, u32[]{:S(2)}) collective-permute-start(bf16[64,3584]{1,0:T(8,128)(2,1)S(1)} %copy-done.1), channel_id=1, source_target_pairs={{0,8},{2,10},{4,12},{6,14},{8,16},{10,18},{12,20},{14,22},{16,24},... | collective-permute-start | bytes 1376264 | tf_op jit(solution)/shard_map/ppermute | solution.py:116
  41.6 20.0 %collective-permute-start.31 = (bf16[2,64,3584]{2,1,0:T(8,128)(2,1)S(1)}, bf16[2,64,3584]{2,1,0:T(8,128)(2,1)S(1)}, u32[]{:S(2)}, u32[]{:S(2)}) collective-permute-start(bf16[2,64,3584]{2,1,0:T(8,128)(2,1)S(1)} %pad_maximum_fusion.12), channel_id=1, source_target_pairs={{0,2},{2,0},{4,6},{6,4},{8,10},{10,8},{12,14},{14,12},{16,18},{18,... | collective-permute-start | bytes 2752520 | tf_op jit(solution)/shard_map/ppermute | solution.py:112
  61.7 97.5 %collective-permute-start.2 = (bf16[3584,512]{1,0:T(8,128)(2,1)S(1)}, bf16[3584,512]{1,0:T(8,128)(2,1)S(1)}, u32[]{:S(2)}, u32[]{:S(2)}) collective-permute-start(bf16[3584,512]{1,0:T(8,128)(2,1)S(1)} %bitcast.284), channel_id=1, source_target_pairs={{0,1},{1,0},{2,3},{3,2},{4,5},{5,4},{6,7},{7,6},{8,9},{9,8},{10,11... | collective-permute-start | bytes 11010056 | tf_op jit(solution)/shard_map/ppermute | solution.py:207
  63.3 103.4 %collective-permute-start.3 = (bf16[512,3584]{1,0:T(8,128)(2,1)S(1)}, bf16[512,3584]{1,0:T(8,128)(2,1)S(1)}, u32[]{:S(2)}, u32[]{:S(2)}) collective-permute-start(bf16[512,3584]{1,0:T(8,128)(2,1)S(1)} %bitcast.293), channel_id=1, source_target_pairs={{0,1},{1,0},{2,3},{3,2},{4,5},{5,4},{6,7},{7,6},{8,9},{9,8},{10,11... | collective-permute-start | bytes 11010056 | tf_op jit(solution)/shard_map/ppermute | solution.py:208
  63.9 63.0 %collective-permute-start.7 = (bf16[64,3584]{1,0:T(8,128)(2,1)S(1)}, bf16[64,3584]{1,0:T(8,128)(2,1)}, u32[]{:S(2)}, u32[]{:S(2)}) collective-permute-start(bf16[64,3584]{1,0:T(8,128)(2,1)S(1)} %collective-permute-done.6), channel_id=1, source_target_pairs={{16,8},{18,10},{20,12},{22,14},{8,0},{10,2},{12,4},{14,6},{17,9},{... | collective-permute-start | bytes 1376264 | tf_op jit(solution)/shard_map/ppermute | solution.py:116
  68.7 53.7 %copy-start.10 = (bf16[64,3584]{1,0:T(8,128)(2,1)}, bf16[64,3584]{1,0:T(8,128)(2,1)S(1)}, u32[]{:S(2)}) copy-start(bf16[64,3584]{1,0:T(8,128)(2,1)S(1)} %collective-permute-done.34) | copy-start | bytes 1376260
  68.7 12.2 %collective-permute-start.16 = (bf16[64,3584]{1,0:T(8,128)(2,1)S(1)}, bf16[64,3584]{1,0:T(8,128)(2,1)S(1)}, u32[]{:S(2)}, u32[]{:S(2)}) collective-permute-start(bf16[64,3584]{1,0:T(8,128)(2,1)S(1)} %get-tuple-element.18), channel_id=1, source_target_pairs={{0,2},{2,0},{4,6},{6,4},{8,10},{10,8},{12,14},{14,12},{16,18},{18,... | collective-permute-start | bytes 1376264 | tf_op jit(solution)/shard_map/ppermute | solution.py:112
  69.3 57.6 %copy-start.16 = (bf16[64,3584]{1,0:T(8,128)(2,1)}, bf16[64,3584]{1,0:T(8,128)(2,1)S(1)}, u32[]{:S(2)}) copy-start(bf16[64,3584]{1,0:T(8,128)(2,1)S(1)} %collective-permute-done.37) | copy-start | bytes 1376260
  70.2 12.2 %collective-permute-start.44 = (bf16[64,3584]{1,0:T(8,128)(2,1)S(1)}, bf16[64,3584]{1,0:T(8,128)(2,1)S(1)}, u32[]{:S(2)}, u32[]{:S(2)}) collective-permute-start(bf16[64,3584]{1,0:T(8,128)(2,1)S(1)} %get-tuple-element.12), channel_id=1, source_target_pairs={{0,4},{2,6},{4,0},{6,2},{8,12},{10,14},{12,8},{14,10},{16,20},{18,... | collective-permute-start | bytes 1376264 | tf_op jit(solution)/shard_map/ppermute | solution.py:112
  81.0 21.2 %collective-permute-start.17 = (bf16[2,64,3584]{2,1,0:T(8,128)(2,1)S(1)}, bf16[2,64,3584]{2,1,0:T(8,128)(2,1)S(1)}, u32[]{:S(2)}, u32[]{:S(2)}) collective-permute-start(bf16[2,64,3584]{2,1,0:T(8,128)(2,1)S(1)} %pad_maximum_fusion.8), channel_id=1, source_target_pairs={{0,4},{2,6},{4,0},{6,2},{8,12},{10,14},{12,8},{14,10},{16,20},{18,... | collective-permute-start | bytes 2752520 | tf_op jit(solution)/shard_map/ppermute | solution.py:112
  82.4 46.4 %collective-permute-start.10 = (bf16[64,3584]{1,0:T(8,128)(2,1)S(1)}, bf16[64,3584]{1,0:T(8,128)(2,1)}, u32[]{:S(2)}, u32[]{:S(2)}) collective-permute-start(bf16[64,3584]{1,0:T(8,128)(2,1)S(1)} %copy-done.15), channel_id=1, source_target_pairs={{8,16},{10,18},{12,20},{14,22},{16,24},{18,26},{20,28},{22,30},{9,... | collective-permute-start | bytes 1376264 | tf_op jit(solution)/shard_map/ppermute | solution.py:116
  102.2 20.2 %collective-permute-start.45 = (bf16[2,64,3584]{2,1,0:T(8,128)(2,1)S(1)}, bf16[2,64,3584]{2,1,0:T(8,128)(2,1)S(1)}, u32[]{:S(2)}, u32[]{:S(2)}) collective-permute-start(bf16[2,64,3584]{2,1,0:T(8,128)(2,1)S(1)} %pad_maximum_fusion.16), channel_id=1, source_target_pairs={{0,2},{2,0},{4,6},{6,4},{8,10},{10,8},{12,14},{14,12},{16,18},{18,... | collective-permute-start | bytes 2752520 | tf_op jit(solution)/shard_map/ppermute | solution.py:112
  122.4 10.7 %collective-permute-start.35 = (bf16[64,3584]{1,0:T(8,128)(2,1)S(1)}, bf16[64,3584]{1,0:T(8,128)(2,1)}, u32[]{:S(2)}, u32[]{:S(2)}) collective-permute-start(bf16[64,3584]{1,0:T(8,128)(2,1)S(1)} %collective-permute-done.34), channel_id=1, source_target_pairs={{16,8},{18,10},{20,12},{22,14},{8,0},{10,2},{12,4},{14,6},{17,9},{... | collective-permute-start | bytes 1376264 | tf_op jit(solution)/shard_map/ppermute | solution.py:116
  126.9 12.9 %collective-permute-start.38 = (bf16[64,3584]{1,0:T(8,128)(2,1)S(1)}, bf16[64,3584]{1,0:T(8,128)(2,1)}, u32[]{:S(2)}, u32[]{:S(2)}) collective-permute-start(bf16[64,3584]{1,0:T(8,128)(2,1)S(1)} %collective-permute-done.37), channel_id=1, source_target_pairs={{8,16},{10,18},{12,20},{14,22},{16,24},{18,26},{20,28},{22,30},{9,... | collective-permute-start | bytes 1376264 | tf_op jit(solution)/shard_map/ppermute | solution.py:116
  128.8 54.3 %collective-permute-start.8 = (bf16[64,3584]{1,0:T(8,128)(2,1)}, bf16[64,3584]{1,0:T(8,128)(2,1)}, u32[]{:S(2)}, u32[]{:S(2)}) collective-permute-start(bf16[64,3584]{1,0:T(8,128)(2,1)} %collective-permute-done.7), channel_id=1, source_target_pairs={{8,0},{10,2},{12,4},{14,6},{9,1},{11,3},{13,5},{15,7}} | collective-permute-start | bytes 1376264 | tf_op jit(solution)/shard_map/ppermute | solution.py:116
  133.1 50.0 %collective-permute-start.11 = (bf16[64,3584]{1,0:T(8,128)(2,1)}, bf16[64,3584]{1,0:T(8,128)(2,1)}, u32[]{:S(2)}, u32[]{:S(2)}) collective-permute-start(bf16[64,3584]{1,0:T(8,128)(2,1)} %collective-permute-done.10), channel_id=1, source_target_pairs={{16,24},{18,26},{20,28},{22,30},{17,25},{19,27},{21,29},{23,31}} | collective-permute-start | bytes 1376264 | tf_op jit(solution)/shard_map/ppermute | solution.py:116
  139.8 8.5 %collective-permute-start.20 = (bf16[64,3584]{1,0:T(8,128)(2,1)S(1)}, bf16[64,3584]{1,0:T(8,128)(2,1)S(1)}, u32[]{:S(2)}, u32[]{:S(2)}) collective-permute-start(bf16[64,3584]{1,0:T(8,128)(2,1)S(1)} %get-tuple-element.16), channel_id=1, source_target_pairs={{0,2},{2,0},{4,6},{6,4},{8,10},{10,8},{12,14},{14,12},{16,18},{18,... | collective-permute-start | bytes 1376264 | tf_op jit(solution)/shard_map/ppermute | solution.py:112
  148.2 8.5 %collective-permute-start.48 = (bf16[64,3584]{1,0:T(8,128)(2,1)S(1)}, bf16[64,3584]{1,0:T(8,128)(2,1)S(1)}, u32[]{:S(2)}, u32[]{:S(2)}) collective-permute-start(bf16[64,3584]{1,0:T(8,128)(2,1)S(1)} %get-tuple-element.10), channel_id=1, source_target_pairs={{0,4},{2,6},{4,0},{6,2},{8,12},{10,14},{12,8},{14,10},{16,20},{18,... | collective-permute-start | bytes 1376264 | tf_op jit(solution)/shard_map/ppermute | solution.py:112
  156.7 46.3 %collective-permute-start.36 = (bf16[64,3584]{1,0:T(8,128)(2,1)}, bf16[64,3584]{1,0:T(8,128)(2,1)}, u32[]{:S(2)}, u32[]{:S(2)}) collective-permute-start(bf16[64,3584]{1,0:T(8,128)(2,1)} %collective-permute-done.35), channel_id=1, source_target_pairs={{8,0},{10,2},{12,4},{14,6},{9,1},{11,3},{13,5},{15,7}} | collective-permute-start | bytes 1376264 | tf_op jit(solution)/shard_map/ppermute | solution.py:116
  159.2 43.9 %collective-permute-start.39 = (bf16[64,3584]{1,0:T(8,128)(2,1)}, bf16[64,3584]{1,0:T(8,128)(2,1)}, u32[]{:S(2)}, u32[]{:S(2)}) collective-permute-start(bf16[64,3584]{1,0:T(8,128)(2,1)} %collective-permute-done.38), channel_id=1, source_target_pairs={{16,24},{18,26},{20,28},{22,30},{17,25},{19,27},{21,29},{23,31}} | collective-permute-start | bytes 1376264 | tf_op jit(solution)/shard_map/ppermute | solution.py:116
  166.7 13.8 %collective-permute-start.21 = (bf16[2,64,3584]{2,1,0:T(8,128)(2,1)}, bf16[2,64,3584]{2,1,0:T(8,128)(2,1)S(1)}, u32[]{:S(2)}, u32[]{:S(2)}) collective-permute-start(bf16[2,64,3584]{2,1,0:T(8,128)(2,1)} %pad_maximum_fusion.10), channel_id=1, source_target_pairs={{0,4},{2,6},{4,0},{6,2},{8,12},{10,14},{12,8},{14,10},{16,20},{18,... | collective-permute-start | bytes 2752520 | tf_op jit(solution)/shard_map/ppermute | solution.py:112
  180.5 18.0 %collective-permute-start.49 = (bf16[2,64,3584]{2,1,0:T(8,128)(2,1)}, bf16[2,64,3584]{2,1,0:T(8,128)(2,1)S(1)}, u32[]{:S(2)}, u32[]{:S(2)}) collective-permute-start(bf16[2,64,3584]{2,1,0:T(8,128)(2,1)} %pad_maximum_fusion.18), channel_id=1, source_target_pairs={{0,2},{2,0},{4,6},{6,4},{8,10},{10,8},{12,14},{14,12},{16,18},{18,... | collective-permute-start | bytes 2752520 | tf_op jit(solution)/shard_map/ppermute | solution.py:112
  185.5 24.3 %collective-permute-start.12 = (bf16[64,3584]{1,0:T(8,128)(2,1)}, bf16[64,3584]{1,0:T(8,128)(2,1)S(1)}, u32[]{:S(2)}, u32[]{:S(2)}) collective-permute-start(bf16[64,3584]{1,0:T(8,128)(2,1)} %get-tuple-element.14), channel_id=1, source_target_pairs={{0,2},{2,0},{4,6},{6,4},{8,10},{10,8},{12,14},{14,12},{16,18},{18,... | collective-permute-start | bytes 1376264 | tf_op jit(solution)/shard_map/ppermute | solution.py:112
  208.3 8.5 %collective-permute-start.40 = (bf16[64,3584]{1,0:T(8,128)(2,1)S(1)}, bf16[64,3584]{1,0:T(8,128)(2,1)S(1)}, u32[]{:S(2)}, u32[]{:S(2)}) collective-permute-start(bf16[64,3584]{1,0:T(8,128)(2,1)S(1)} %get-tuple-element.8), channel_id=1, source_target_pairs={{0,4},{2,6},{4,0},{6,2},{8,12},{10,14},{12,8},{14,10},{16,20},{18,... | collective-permute-start | bytes 1376264 | tf_op jit(solution)/shard_map/ppermute | solution.py:112
  211.2 15.5 %collective-permute-start.13 = (bf16[2,64,3584]{2,1,0:T(8,128)(2,1)S(1)}, bf16[2,64,3584]{2,1,0:T(8,128)(2,1)S(1)}, u32[]{:S(2)}, u32[]{:S(2)}) collective-permute-start(bf16[2,64,3584]{2,1,0:T(8,128)(2,1)S(1)} %pad_maximum_fusion.6), channel_id=1, source_target_pairs={{0,4},{2,6},{4,0},{6,2},{8,12},{10,14},{12,8},{14,10},{16,20},{18,... | collective-permute-start | bytes 2752520 | tf_op jit(solution)/shard_map/ppermute | solution.py:112
  216.9 13.8 %collective-permute-start.41 = (bf16[2,64,3584]{2,1,0:T(8,128)(2,1)S(1)}, bf16[2,64,3584]{2,1,0:T(8,128)(2,1)S(1)}, u32[]{:S(2)}, u32[]{:S(2)}) collective-permute-start(bf16[2,64,3584]{2,1,0:T(8,128)(2,1)S(1)} %pad_maximum_fusion.14), channel_id=1, source_target_pairs={{0,2},{2,0},{4,6},{6,4},{8,10},{10,8},{12,14},{14,12},{16,18},{18,... | collective-permute-start | bytes 2752520 | tf_op jit(solution)/shard_map/ppermute | solution.py:112
  316.4 66.4 %collective-permute-start.32 = (bf16[2,64,3584]{2,1,0:T(8,128)(2,1)S(1)}, bf16[2,64,3584]{2,1,0:T(8,128)(2,1)}, u32[]{:S(2)}, u32[]{:S(2)}) collective-permute-start(bf16[2,64,3584]{2,1,0:T(8,128)(2,1)S(1)} %pad_maximum_fusion.13), channel_id=1, source_target_pairs={{0,2},{2,0},{4,6},{6,4},{8,10},{10,8},{12,14},{14,12},{16,18},{18,... | collective-permute-start | bytes 2752520 | tf_op jit(solution)/shard_map/ppermute | solution.py:112
  325.2 60.8 %collective-permute-start.46 = (bf16[2,64,3584]{2,1,0:T(8,128)(2,1)}, bf16[2,64,3584]{2,1,0:T(8,128)(2,1)}, u32[]{:S(2)}, u32[]{:S(2)}) collective-permute-start(bf16[2,64,3584]{2,1,0:T(8,128)(2,1)} %pad_maximum_fusion.17), channel_id=1, source_target_pairs={{0,2},{2,0},{4,6},{6,4},{8,10},{10,8},{12,14},{14,12},{16,18},{18,... | collective-permute-start | bytes 2752520 | tf_op jit(solution)/shard_map/ppermute | solution.py:112
  339.4 47.9 %collective-permute-start.50 = (bf16[2,64,3584]{2,1,0:T(8,128)(2,1)S(1)}, bf16[2,64,3584]{2,1,0:T(8,128)(2,1)S(1)}, u32[]{:S(2)}, u32[]{:S(2)}) collective-permute-start(bf16[2,64,3584]{2,1,0:T(8,128)(2,1)S(1)} %pad_maximum_fusion.19), channel_id=1, source_target_pairs={{0,2},{2,0},{4,6},{6,4},{8,10},{10,8},{12,14},{14,12},{16,18},{18,... | collective-permute-start | bytes 2752520 | tf_op jit(solution)/shard_map/ppermute | solution.py:112
  340.1 49.3 %collective-permute-start.42 = (bf16[2,64,3584]{2,1,0:T(8,128)(2,1)S(1)}, bf16[2,64,3584]{2,1,0:T(8,128)(2,1)}, u32[]{:S(2)}, u32[]{:S(2)}) collective-permute-start(bf16[2,64,3584]{2,1,0:T(8,128)(2,1)S(1)} %pad_maximum_fusion.15), channel_id=1, source_target_pairs={{0,2},{2,0},{4,6},{6,4},{8,10},{10,8},{12,14},{14,12},{16,18},{18,... | collective-permute-start | bytes 2752520 | tf_op jit(solution)/shard_map/ppermute | solution.py:112
  346.1 44.5 %collective-permute-start.4 = (bf16[2,64,3584]{2,1,0:T(8,128)(2,1)S(1)}, bf16[2,64,3584]{2,1,0:T(8,128)(2,1)}, u32[]{:S(2)}, u32[]{:S(2)}) collective-permute-start(bf16[2,64,3584]{2,1,0:T(8,128)(2,1)S(1)} %pad_maximum_fusion.5), channel_id=1, source_target_pairs={{0,4},{2,6},{4,0},{6,2},{8,12},{10,14},{12,8},{14,10},{16,20},{18,... | collective-permute-start | bytes 2752520 | tf_op jit(solution)/shard_map/ppermute | solution.py:112
  382.8 20.0 %collective-permute-start.18 = (bf16[2,64,3584]{2,1,0:T(8,128)(2,1)S(1)}, bf16[2,64,3584]{2,1,0:T(8,128)(2,1)S(1)}, u32[]{:S(2)}, u32[]{:S(2)}) collective-permute-start(bf16[2,64,3584]{2,1,0:T(8,128)(2,1)S(1)} %pad_maximum_fusion.9), channel_id=1, source_target_pairs={{0,4},{2,6},{4,0},{6,2},{8,12},{10,14},{12,8},{14,10},{16,20},{18,... | collective-permute-start | bytes 2752520 | tf_op jit(solution)/shard_map/ppermute | solution.py:112
  386.0 42.6 %collective-permute-start.22 = (bf16[2,64,3584]{2,1,0:T(8,128)(2,1)S(1)}, bf16[2,64,3584]{2,1,0:T(8,128)(2,1)S(1)}, u32[]{:S(2)}, u32[]{:S(2)}) collective-permute-start(bf16[2,64,3584]{2,1,0:T(8,128)(2,1)S(1)} %pad_maximum_fusion.11), channel_id=1, source_target_pairs={{0,4},{2,6},{4,0},{6,2},{8,12},{10,14},{12,8},{14,10},{16,20},{18,... | collective-permute-start | bytes 2752520 | tf_op jit(solution)/shard_map/ppermute | solution.py:112
  387.3 41.1 %collective-permute-start.14 = (bf16[2,64,3584]{2,1,0:T(8,128)(2,1)S(1)}, bf16[2,64,3584]{2,1,0:T(8,128)(2,1)S(1)}, u32[]{:S(2)}, u32[]{:S(2)}) collective-permute-start(bf16[2,64,3584]{2,1,0:T(8,128)(2,1)S(1)} %pad_maximum_fusion.7), channel_id=1, source_target_pairs={{0,4},{2,6},{4,0},{6,2},{8,12},{10,14},{12,8},{14,10},{16,20},{18,... | collective-permute-start | bytes 2752520 | tf_op jit(solution)/shard_map/ppermute | solution.py:112
  389.4 135.7 %collective-permute-start.58 = (bf16[3584,512]{1,0:T(8,128)(2,1)S(1)}, bf16[3584,512]{1,0:T(8,128)(2,1)S(1)}, u32[]{:S(2)}, u32[]{:S(2)}) collective-permute-start(bf16[3584,512]{1,0:T(8,128)(2,1)S(1)} %copy-done.45), channel_id=1, source_target_pairs={{0,1},{1,0},{2,3},{3,2},{4,5},{5,4},{6,7},{7,6},{8,9},{9,8},{10,11... | collective-permute-start | bytes 11010056 | tf_op jit(solution)/shard_map/ppermute | solution.py:240
  390.6 143.3 %collective-permute-start.59 = (bf16[512,3584]{1,0:T(8,128)(2,1)}, bf16[512,3584]{1,0:T(8,128)(2,1)S(1)}, u32[]{:S(2)}, u32[]{:S(2)}) collective-permute-start(bf16[512,3584]{1,0:T(8,128)(2,1)} %convolution_convert_fusion), channel_id=1, source_target_pairs={{0,1},{1,0},{2,3},{3,2},{4,5},{5,4},{6,7},{7,6},{8,9},{9,8},{10,11... | collective-permute-start | bytes 11010056 | tf_op jit(solution)/shard_map/ppermute | solution.py:239
  392.3 72.6 %copy-start.28 = (bf16[2,64,3584]{2,1,0:T(8,128)(2,1)S(1)}, bf16[2,64,3584]{2,1,0:T(8,128)(2,1)}, u32[]{:S(2)}) copy-start(bf16[2,64,3584]{2,1,0:T(8,128)(2,1)} %copy-done.27) | copy-start | bytes 2752516
  402.8 42.1 %collective-permute-start.51 = (bf16[64,3584]{1,0:T(8,128)(2,1)S(1)}, bf16[64,3584]{1,0:T(8,128)(2,1)S(1)}, u32[]{:S(2)}, u32[]{:S(2)}) collective-permute-start(bf16[64,3584]{1,0:T(8,128)(2,1)S(1)} %fusion.102), channel_id=1, source_target_pairs={{0,4},{2,6},{4,0},{6,2},{8,12},{10,14},{12,8},{14,10},{16,20},{18,... | collective-permute-start | bytes 1376264 | tf_op jit(solution)/shard_map/ppermute | solution.py:112
  428.4 13.1 %collective-permute-start.43 = (bf16[64,3584]{1,0:T(8,128)(2,1)S(1)}, bf16[64,3584]{1,0:T(8,128)(2,1)S(1)}, u32[]{:S(2)}, u32[]{:S(2)}) collective-permute-start(bf16[64,3584]{1,0:T(8,128)(2,1)S(1)} %fusion.106), channel_id=1, source_target_pairs={{0,4},{2,6},{4,0},{6,2},{8,12},{10,14},{12,8},{14,10},{16,20},{18,... | collective-permute-start | bytes 1376264 | tf_op jit(solution)/shard_map/ppermute | solution.py:112
  428.6 15.5 %collective-permute-start.15 = (bf16[64,3584]{1,0:T(8,128)(2,1)S(1)}, bf16[64,3584]{1,0:T(8,128)(2,1)S(1)}, u32[]{:S(2)}, u32[]{:S(2)}) collective-permute-start(bf16[64,3584]{1,0:T(8,128)(2,1)S(1)} %fusion.114), channel_id=1, source_target_pairs={{0,2},{2,0},{4,6},{6,4},{8,10},{10,8},{12,14},{14,12},{16,18},{18,... | collective-permute-start | bytes 1376264 | tf_op jit(solution)/shard_map/ppermute | solution.py:112
  442.7 20.2 %collective-permute-start.55 = (bf16[64,3584]{1,0:T(8,128)(2,1)S(1)}, bf16[64,3584]{1,0:T(8,128)(2,1)S(1)}, u32[]{:S(2)}, u32[]{:S(2)}) collective-permute-start(bf16[64,3584]{1,0:T(8,128)(2,1)S(1)} %add_convert_fusion.7), channel_id=1, source_target_pairs={{24,16},{26,18},{28,20},{30,22},{25,17},{27,19},{29,21},{31,23}} | collective-permute-start | bytes 1376264 | tf_op jit(solution)/shard_map/ppermute | solution.py:116
  444.0 20.2 %collective-permute-start.52 = (bf16[64,3584]{1,0:T(8,128)(2,1)S(1)}, bf16[64,3584]{1,0:T(8,128)(2,1)S(1)}, u32[]{:S(2)}, u32[]{:S(2)}) collective-permute-start(bf16[64,3584]{1,0:T(8,128)(2,1)S(1)} %add_convert_fusion.7), channel_id=1, source_target_pairs={{0,8},{2,10},{4,12},{6,14},{1,9},{3,11},{5,13},{7,15}} | collective-permute-start | bytes 1376264 | tf_op jit(solution)/shard_map/ppermute | solution.py:116
  444.9 20.3 %collective-permute-start.23 = (bf16[64,3584]{1,0:T(8,128)(2,1)S(1)}, bf16[64,3584]{1,0:T(8,128)(2,1)S(1)}, u32[]{:S(2)}, u32[]{:S(2)}) collective-permute-start(bf16[64,3584]{1,0:T(8,128)(2,1)S(1)} %fusion.110), channel_id=1, source_target_pairs={{0,2},{2,0},{4,6},{6,4},{8,10},{10,8},{12,14},{14,12},{16,18},{18,... | collective-permute-start | bytes 1376264 | tf_op jit(solution)/shard_map/ppermute | solution.py:112
  462.9 14.9 %collective-permute-start.27 = (bf16[64,3584]{1,0:T(8,128)(2,1)S(1)}, bf16[64,3584]{1,0:T(8,128)(2,1)S(1)}, u32[]{:S(2)}, u32[]{:S(2)}) collective-permute-start(bf16[64,3584]{1,0:T(8,128)(2,1)S(1)} %add_convert_fusion.14), channel_id=1, source_target_pairs={{24,16},{26,18},{28,20},{30,22},{25,17},{27,19},{29,21},{31,23}} | collective-permute-start | bytes 1376264 | tf_op jit(solution)/shard_map/ppermute | solution.py:116
  464.2 14.9 %collective-permute-start.24 = (bf16[64,3584]{1,0:T(8,128)(2,1)S(1)}, bf16[64,3584]{1,0:T(8,128)(2,1)S(1)}, u32[]{:S(2)}, u32[]{:S(2)}) collective-permute-start(bf16[64,3584]{1,0:T(8,128)(2,1)S(1)} %add_convert_fusion.14), channel_id=1, source_target_pairs={{0,8},{2,10},{4,12},{6,14},{1,9},{3,11},{5,13},{7,15}} | collective-permute-start | bytes 1376264 | tf_op jit(solution)/shard_map/ppermute | solution.py:116
  465.2 18.8 %collective-permute-start.47 = (bf16[64,3584]{1,0:T(8,128)(2,1)S(1)}, bf16[64,3584]{1,0:T(8,128)(2,1)S(1)}, u32[]{:S(2)}, u32[]{:S(2)}) collective-permute-start(bf16[64,3584]{1,0:T(8,128)(2,1)S(1)} %fusion.104), channel_id=1, source_target_pairs={{0,4},{2,6},{4,0},{6,2},{8,12},{10,14},{12,8},{14,10},{16,20},{18,... | collective-permute-start | bytes 1376264 | tf_op jit(solution)/shard_map/ppermute | solution.py:112
  477.8 10.4 %collective-permute-start.53 = (bf16[64,3584]{1,0:T(8,128)(2,1)S(1)}, bf16[64,3584]{1,0:T(8,128)(2,1)S(1)}, u32[]{:S(2)}, u32[]{:S(2)}) collective-permute-start(bf16[64,3584]{1,0:T(8,128)(2,1)S(1)} %get-tuple-element.23), channel_id=1, source_target_pairs={{0,8},{2,10},{4,12},{6,14},{8,16},{10,18},{12,20},{14,22},{1,9},{3... | collective-permute-start | bytes 1376264 | tf_op jit(solution)/shard_map/ppermute | solution.py:116
  479.1 12.8 %collective-permute-start.56 = (bf16[64,3584]{1,0:T(8,128)(2,1)S(1)}, bf16[64,3584]{1,0:T(8,128)(2,1)S(1)}, u32[]{:S(2)}, u32[]{:S(2)}) collective-permute-start(bf16[64,3584]{1,0:T(8,128)(2,1)S(1)} %get-tuple-element.24), channel_id=1, source_target_pairs={{24,16},{26,18},{28,20},{30,22},{16,8},{18,10},{20,12},{22,14},{25... | collective-permute-start | bytes 1376264 | tf_op jit(solution)/shard_map/ppermute | solution.py:116
  484.0 11.5 %collective-permute-start.19 = (bf16[64,3584]{1,0:T(8,128)(2,1)S(1)}, bf16[64,3584]{1,0:T(8,128)(2,1)S(1)}, u32[]{:S(2)}, u32[]{:S(2)}) collective-permute-start(bf16[64,3584]{1,0:T(8,128)(2,1)S(1)} %fusion.112), channel_id=1, source_target_pairs={{0,2},{2,0},{4,6},{6,4},{8,10},{10,8},{12,14},{14,12},{16,18},{18,... | collective-permute-start | bytes 1376264 | tf_op jit(solution)/shard_map/ppermute | solution.py:112
  488.2 10.4 %collective-permute-start.25 = (bf16[64,3584]{1,0:T(8,128)(2,1)S(1)}, bf16[64,3584]{1,0:T(8,128)(2,1)S(1)}, u32[]{:S(2)}, u32[]{:S(2)}) collective-permute-start(bf16[64,3584]{1,0:T(8,128)(2,1)S(1)} %get-tuple-element.25), channel_id=1, source_target_pairs={{0,8},{2,10},{4,12},{6,14},{8,16},{10,18},{12,20},{14,22},{1,9},{3... | collective-permute-start | bytes 1376264 | tf_op jit(solution)/shard_map/ppermute | solution.py:116
  491.9 10.4 %collective-permute-start.28 = (bf16[64,3584]{1,0:T(8,128)(2,1)S(1)}, bf16[64,3584]{1,0:T(8,128)(2,1)S(1)}, u32[]{:S(2)}, u32[]{:S(2)}) collective-permute-start(bf16[64,3584]{1,0:T(8,128)(2,1)S(1)} %get-tuple-element.26), channel_id=1, source_target_pairs={{24,16},{26,18},{28,20},{30,22},{16,8},{18,10},{20,12},{22,14},{25... | collective-permute-start | bytes 1376264 | tf_op jit(solution)/shard_map/ppermute | solution.py:116
  495.6 9.4 %collective-permute-start.33 = (bf16[64,3584]{1,0:T(8,128)(2,1)S(1)}, bf16[64,3584]{1,0:T(8,128)(2,1)S(1)}, u32[]{:S(2)}, u32[]{:S(2)}) collective-permute-start(bf16[64,3584]{1,0:T(8,128)(2,1)S(1)} %fusion.108), channel_id=1, source_target_pairs={{0,4},{2,6},{4,0},{6,2},{8,12},{10,14},{12,8},{14,10},{16,20},{18,... | collective-permute-start | bytes 1376264 | tf_op jit(solution)/shard_map/ppermute | solution.py:112
  498.6 10.4 %collective-permute-start.54 = (bf16[64,3584]{1,0:T(8,128)(2,1)S(1)}, bf16[64,3584]{1,0:T(8,128)(2,1)S(1)}, u32[]{:S(2)}, u32[]{:S(2)}) collective-permute-start(bf16[64,3584]{1,0:T(8,128)(2,1)S(1)} %get-tuple-element.19), channel_id=1, source_target_pairs={{0,8},{2,10},{4,12},{6,14},{8,16},{10,18},{12,20},{14,22},{16,24},... | collective-permute-start | bytes 1376264 | tf_op jit(solution)/shard_map/ppermute | solution.py:116
  502.3 10.4 %collective-permute-start.57 = (bf16[64,3584]{1,0:T(8,128)(2,1)S(1)}, bf16[64,3584]{1,0:T(8,128)(2,1)S(1)}, u32[]{:S(2)}, u32[]{:S(2)}) collective-permute-start(bf16[64,3584]{1,0:T(8,128)(2,1)S(1)} %get-tuple-element.20), channel_id=1, source_target_pairs={{24,16},{26,18},{28,20},{30,22},{16,8},{18,10},{20,12},{22,14},{8,... | collective-permute-start | bytes 1376264 | tf_op jit(solution)/shard_map/ppermute | solution.py:116
  504.9 12.0 %collective-permute-start.5 = (bf16[64,3584]{1,0:T(8,128)(2,1)S(1)}, bf16[64,3584]{1,0:T(8,128)(2,1)S(1)}, u32[]{:S(2)}, u32[]{:S(2)}) collective-permute-start(bf16[64,3584]{1,0:T(8,128)(2,1)S(1)} %fusion.116), channel_id=1, source_target_pairs={{0,2},{2,0},{4,6},{6,4},{8,10},{10,8},{12,14},{14,12},{16,18},{18,... | collective-permute-start | bytes 1376264 | tf_op jit(solution)/shard_map/ppermute | solution.py:112
  508.9 10.4 %collective-permute-start.26 = (bf16[64,3584]{1,0:T(8,128)(2,1)S(1)}, bf16[64,3584]{1,0:T(8,128)(2,1)S(1)}, u32[]{:S(2)}, u32[]{:S(2)}) collective-permute-start(bf16[64,3584]{1,0:T(8,128)(2,1)S(1)} %get-tuple-element.21), channel_id=1, source_target_pairs={{0,8},{2,10},{4,12},{6,14},{8,16},{10,18},{12,20},{14,22},{16,24},... | collective-permute-start | bytes 1376264 | tf_op jit(solution)/shard_map/ppermute | solution.py:116
  512.7 10.4 %collective-permute-start.29 = (bf16[64,3584]{1,0:T(8,128)(2,1)S(1)}, bf16[64,3584]{1,0:T(8,128)(2,1)S(1)}, u32[]{:S(2)}, u32[]{:S(2)}) collective-permute-start(bf16[64,3584]{1,0:T(8,128)(2,1)S(1)} %get-tuple-element.22), channel_id=1, source_target_pairs={{24,16},{26,18},{28,20},{30,22},{16,8},{18,10},{20,12},{22,14},{8,... | collective-permute-start | bytes 1376264 | tf_op jit(solution)/shard_map/ppermute | solution.py:116
  (42 other events, 451.8 us)
where the time goes:
time: 548 us; the launch traced here: 543 us
  waiting for transfers between devices  226 us (41%)
  matrix products  101 us (18%)
  starting transfers between devices  82.1 us (15%)
  blocking collectives  67 us (12%)
  other arithmetic  35.1 us (6%)
  local copies, waits for them, and re-layouts  30.5 us (6%)
    ppermute x32, waiting for transfers between devices, swapped(): lax.ppermute(array, 'expert', tuple(((i, i ^ bit) for i in range(16))))  169 us
    ppermute x24, waiting for transfers between devices, shifted(): lax.ppermute(array, 'expert', tuple(((i, i + 4 * step) for z in senders f...  56.8 us
    ppermute x24, starting transfers between devices, shifted(): lax.ppermute(array, 'expert', tuple(((i, i + 4 * step) for z in senders f...  53.6 us
    dot_general x8, matrix products, transposed_dot(): lax.dot_general(rows, weights, (((1,), (1,)), ((), ())), preferred_elemen...  36.7 us
    dot_general x4, matrix products, outer(): lax.dot_general(rows, columns, (((0,), (0,)), ((), ())), preferred_elemen...  34.7 us
    all_gather x1, blocking collectives, dense_shards(): lax.all_gather(inner, 'expert', axis=0, tiled=True)  33.8 us
    all_gather x1, blocking collectives, dense_shards(): lax.all_gather(gate_of, 'expert', axis=0, tiled=True)  33.2 us
    ppermute x32, starting transfers between devices, swapped(): lax.ppermute(array, 'expert', tuple(((i, i ^ bit) for i in range(16))))  27.2 us
  transfers between devices with their start and end apart: 60, of which 27 were waited for; matrix products, arithmetic and copies ran while one was open for 25% of the time, Pallas kernels for 0%

commit v1 on v0

--- a/solution.py
+++ b/solution.py
@@ -5,6 +5,19 @@
 
 GELU_C = 0.7978845608028654
 GELU_A = 0.044715
+
+
+def collect(x, axis, dim):
+    ways = lax.axis_size(axis)
+    up = [(d, (d + 1) % ways) for d in range(ways)]
+    down = [(d, (d - 1) % ways) for d in range(ways)]
+    earlier, later = ([x], [x])
+    for _ in range(ways // 2):
+        earlier.append(lax.ppermute(earlier[-1], axis, up))
+    for _ in range((ways - 1) // 2):
+        later.append(lax.ppermute(later[-1], axis, down))
+    line = jnp.concatenate([*earlier[::-1], *later[1:]], axis=dim)
+    return jnp.roll(line, (lax.axis_index(axis) - ways // 2) * x.shape[dim], axis=dim)
 
 
 def gelu_value(hidden):
@@ -225,9 +238,7 @@
     d_tokens = scattered_layers(dx_columns, layer)
     order = jnp.concatenate(sources)
     inner = jnp.zeros((owners, tok_rows), jnp.float32).at[order].set(jnp.concatenate(inners))
-    inner_all = lax.all_gather(inner, "expert", axis=0, tiled=True).reshape(
-        owners, owners, tok_rows
-    )
+    inner_all = collect(inner, "expert", 0).reshape(owners, owners, tok_rows)
     home = lax.dynamic_index_in_dim(inner_all, mine, axis=1, keepdims=False)
     d_gates = jnp.sum(jnp.where(named, home.T[:, None, :], 0.0), axis=2)
     all_x, all_u = (jnp.concatenate(slots_x), jnp.concatenate(slots_u))

time: 548 us -> 555 us (1.013)
  starting transfers between devices: 82.1 us -> 121 us
  blocking collectives: 67 us -> 46.4 us
  local copies, waits for them, and re-layouts: 30.5 us -> 17 us
  matrix products: 101 us -> 87.8 us
  waiting for transfers between devices: 226 us -> 233 us
    all_gather x1 -> x0, blocking collectives: 33.8 us -> none  [dense_shards(): lax.all_gather(inner, 'expert', axis=0, tiled=True)]
    ppermute x0 -> x15, starting transfers between devices: none -> 22.2 us  [the longest x7 11.7 us: collect(): later.append(lax.ppermute(later[-1], axis, down))]
    ppermute x0 -> x15, waiting for transfers between devices: none -> 15.2 us  [the longest x8 10.1 us: collect(): earlier.append(lax.ppermute(earlier[-1], axis, up))]
    unnamed x116 -> x159, local copies, waits for them, and re-layouts: 24 us -> 10.4 us
    all_gather x1, blocking collectives: 33.2 us -> 46.4 us  [dense_shards(): lax.all_gather(gate_of, 'expert', axis=0, tiled=True)]
    ppermute x24, waiting for transfers between devices: 56.8 us -> 43.6 us  [shifted(): lax.ppermute(array, 'expert', tuple(((i, i + 4 * step) for z in senders f...]
    ppermute x32, starting transfers between devices: 27.2 us -> 40.1 us  [swapped(): lax.ppermute(array, 'expert', tuple(((i, i ^ bit) for i in range(16))))]
    dot_general x4, matrix products: 18.9 us -> 12.2 us  [dense_shards(): out_part = jnp.dot(gated[s], down_full, preferred_element_type=jnp.float32)]
  transfers between devices with their start and end apart: 60 -> 75, of which waited for: 27 -> 40; matrix products, arithmetic and copies ran while one was open for 25% -> 21% of each run, Pallas kernels for 0% -> 0%
where the time goes in v1:
time: 555 us; the launch traced here: 547 us
  waiting for transfers between devices  233 us (42%)
  starting transfers between devices  121 us (22%)
  matrix products  87.8 us (16%)
  blocking collectives  46.4 us (8%)
  other arithmetic  38.3 us (7%)
  local copies, waits for them, and re-layouts  17 us (3%)
    ppermute x32, waiting for transfers between devices, swapped(): lax.ppermute(array, 'expert', tuple(((i, i ^ bit) for i in range(16))))  174 us
    ppermute x24, starting transfers between devices, shifted(): lax.ppermute(array, 'expert', tuple(((i, i + 4 * step) for z in senders f...  57.7 us
    all_gather x1, blocking collectives, dense_shards(): lax.all_gather(gate_of, 'expert', axis=0, tiled=True)  46.4 us
    ppermute x24, waiting for transfers between devices, shifted(): lax.ppermute(array, 'expert', tuple(((i, i + 4 * step) for z in senders f...  43.6 us
    ppermute x32, starting transfers between devices, swapped(): lax.ppermute(array, 'expert', tuple(((i, i ^ bit) for i in range(16))))  40.1 us
    dot_general x8, matrix products, transposed_dot(): lax.dot_general(rows, weights, (((1,), (1,)), ((), ())), preferred_elemen...  32.3 us
    dot_general x4, matrix products, outer(): lax.dot_general(rows, columns, (((0,), (0,)), ((), ())), preferred_elemen...  29.6 us
    convert_element_type x16, other arithmetic, add_rows(): return total.astype(jnp.bfloat16)  15 us
  transfers between devices with their start and end apart: 75, of which 40 were waited for; matrix products, arithmetic and copies ran while one was open for 21% of the time, Pallas kernels for 0%

profile of v1, /device:TPU:20, one launch (start us, length us, event | category | flops | bytes accessed | tf_op | source)
XLA Modules:
  0.0 546.5 jit_solution(10034245544902155205)
XLA Ops:
  0.6 2.5 collective-permute-start.6
  4.7 3.5 collective-permute-start.9
  8.2 2.3 collective-permute-start.34
  17.1 7.2 %collective-permute-done.30 = bf16[64,3584]{1,0:T(8,128)(2,1)S(1)} collective-permute-done((bf16[64,3584]{1,0:T(8,128)(2,1)}, bf16[64,3584]{1,0:T(8,128)(2,1)S(1)}, u32[]{:S(2)}, u32[]{:S(2)}) %collective-permute-start.30) | collective-permute-done | bytes 458784 | tf_op jit(solution)/shard_map/ppermute | solution.py:125
  24.3 3.5 collective-permute-start.37
  27.9 13.7 %collective-permute-done.1 = bf16[2,64,3584]{2,1,0:T(8,128)(2,1)S(1)} collective-permute-done((bf16[2,64,3584]{2,1,0:T(8,128)(2,1)S(1)}, bf16[2,64,3584]{2,1,0:T(8,128)(2,1)S(1)}, u32[]{:S(2)}, u32[]{:S(2)}) %collective-permute-start.1) | collective-permute-done | bytes 917536 | tf_op jit(solution)/shard_map/ppermute | solution.py:125
  42.2 19.4 %collective-permute-done.31 = bf16[2,64,3584]{2,1,0:T(8,128)(2,1)S(1)} collective-permute-done((bf16[2,64,3584]{2,1,0:T(8,128)(2,1)S(1)}, bf16[2,64,3584]{2,1,0:T(8,128)(2,1)S(1)}, u32[]{:S(2)}, u32[]{:S(2)}) %collective-permute-start.31) | collective-permute-done | bytes 917536 | tf_op jit(solution)/shard_map/ppermute | solution.py:125
  62.4 3.2 collective-permute-start.7
  67.3 10.7 %collective-permute-done.16 = bf16[64,3584]{1,0:T(8,128)(2,1)S(1)} collective-permute-done((bf16[64,3584]{1,0:T(8,128)(2,1)S(1)}, bf16[64,3584]{1,0:T(8,128)(2,1)S(1)}, u32[]{:S(2)}, u32[]{:S(2)}) %collective-permute-start.16) | collective-permute-done | bytes 458784 | tf_op jit(solution)/shard_map/ppermute | solution.py:125
  80.9 18.4 %collective-permute-done.17 = bf16[2,64,3584]{2,1,0:T(8,128)(2,1)S(1)} collective-permute-done((bf16[2,64,3584]{2,1,0:T(8,128)(2,1)S(1)}, bf16[2,64,3584]{2,1,0:T(8,128)(2,1)S(1)}, u32[]{:S(2)}, u32[]{:S(2)}) %collective-permute-start.17) | collective-permute-done | bytes 917536 | tf_op jit(solution)/shard_map/ppermute | solution.py:125
  99.9 19.6 %collective-permute-done.45 = bf16[2,64,3584]{2,1,0:T(8,128)(2,1)S(1)} collective-permute-done((bf16[2,64,3584]{2,1,0:T(8,128)(2,1)S(1)}, bf16[2,64,3584]{2,1,0:T(8,128)(2,1)S(1)}, u32[]{:S(2)}, u32[]{:S(2)}) %collective-permute-start.45) | collective-permute-done | bytes 917536 | tf_op jit(solution)/shard_map/ppermute | solution.py:125
  119.5 3.0 collective-permute-start.35
  131.1 4.3 collective-permute-done.38
  138.2 5.7 %collective-permute-done.20 = bf16[64,3584]{1,0:T(8,128)(2,1)S(1)} collective-permute-done((bf16[64,3584]{1,0:T(8,128)(2,1)S(1)}, bf16[64,3584]{1,0:T(8,128)(2,1)S(1)}, u32[]{:S(2)}, u32[]{:S(2)}) %collective-permute-start.20) | collective-permute-done | bytes 458784 | tf_op jit(solution)/shard_map/ppermute | solution.py:125
  145.5 6.9 %collective-permute-done.48 = bf16[64,3584]{1,0:T(8,128)(2,1)S(1)} collective-permute-done((bf16[64,3584]{1,0:T(8,128)(2,1)S(1)}, bf16[64,3584]{1,0:T(8,128)(2,1)S(1)}, u32[]{:S(2)}, u32[]{:S(2)}) %collective-permute-start.48) | collective-permute-done | bytes 458784 | tf_op jit(solution)/shard_map/ppermute | solution.py:125
  154.9 5.8 %collective-permute-start.39 = (bf16[64,3584]{1,0:T(8,128)(2,1)}, bf16[64,3584]{1,0:T(8,128)(2,1)}, u32[]{:S(2)}, u32[]{:S(2)}) collective-permute-start(bf16[64,3584]{1,0:T(8,128)(2,1)} %collective-permute-done.38), channel_id=1, source_target_pairs={{16,24},{18,26},{20,28},{22,30},{17,25},{19,27},{21,29},{23,31}} | collective-permute-start | bytes 1376264 | tf_op jit(solution)/shard_map/ppermute | solution.py:129
  163.4 3.2 multiply_reduce_fusion.3
  166.6 5.2 fusion.18
  171.9 6.7 %multiply_reduce_fusion.2 = (f32[256]{0:T(256)S(1)}, f32[256,1024]{1,0:T(8,128)}) fusion(f32[256,1024]{1,0:T(8,128)} %fusion.18, bf16[512,3584]{1,0:T(8,128)(2,1)} %copy-done.43, bf16[512,3584]{1,0:T(8,128)(2,1)} %bitcast.292, bf16[64,3584]{1,0:T(8,128)(2,1)} %get-tuple-element.58, bf16[64,3584]{1,0:T(8,128)(2,1)S(1)} %collective-permute-done.44, ...), kind=kOutput, calls=%fused_computation.133 | convolution fusion | flops 1903689472 | bytes 11273216 | tf_op jit(solution)/shard_map/dot_general | solution.py:186
  184.4 12.5 %collective-permute-done.49 = bf16[2,64,3584]{2,1,0:T(8,128)(2,1)S(1)} collective-permute-done((bf16[2,64,3584]{2,1,0:T(8,128)(2,1)}, bf16[2,64,3584]{2,1,0:T(8,128)(2,1)S(1)}, u32[]{:S(2)}, u32[]{:S(2)}) %collective-permute-start.49) | collective-permute-done | bytes 917536 | tf_op jit(solution)/shard_map/ppermute | solution.py:125
  206.5 3.1 multiply_reduce_fusion.1
  212.5 7.6 %collective-permute-done.13 = bf16[2,64,3584]{2,1,0:T(8,128)(2,1)S(1)} collective-permute-done((bf16[2,64,3584]{2,1,0:T(8,128)(2,1)}, bf16[2,64,3584]{2,1,0:T(8,128)(2,1)S(1)}, u32[]{:S(2)}, u32[]{:S(2)}) %collective-permute-start.13) | collective-permute-done | bytes 917536 | tf_op jit(solution)/shard_map/ppermute | solution.py:125
  220.2 5.0 collective-permute-done.41
  225.3 4.3 fusion.10
  229.6 4.8 multiply_reduce_fusion
  235.9 3.7 collective-permute-done.58
  239.7 2.9 collective-permute-start.66
  245.1 2.9 collective-permute-start.67
  257.9 2.4 collective-permute-start.63
  263.0 2.7 collective-permute-start.64
  268.5 2.7 collective-permute-start.65
  274.1 3.6 collective-permute-done.72
  278.6 46.4 %all-gather = f32[16,64,16]{1,2,0:T(8,128)S(1)} all-gather(f32[1,64,16]{1,2,0:T(8,128)S(1)} %bitcast.281), channel_id=1, replica_groups=mesh['expert'=16,'tok'=2] {'expert'}, dimensions={0}, use_global_device_ids=true | all-gather | bytes 69632 | tf_op jit(solution)/shard_map/all_gather | solution.py:207
  329.6 5.4 convolution_convert_fusion.5
  335.2 2.4 collective-permute-start.32
  338.5 2.6 convolution_convert_fusion.3
  344.7 2.4 convolution_convert_fusion.4
  347.2 4.3 convolution_convert_fusion.2
  355.6 2.3 convolution_convert_fusion.9
  359.0 2.3 convolution_convert_fusion.7
  361.6 2.3 convolution_convert_fusion.8
  364.0 5.4 convolution_convert_fusion.6
  371.6 5.9 %convolution_convert_fusion = bf16[512,3584]{1,0:T(8,128)(2,1)} fusion(bf16[1024,3584]{1,0:T(8,128)(2,1)S(1)} %bitcast.260, bf16[1024,1024]{1,0:T(8,128)(2,1)S(1)} %pad_maximum_fusion.3), kind=kOutput, calls=%fused_computation.9 | convolution fusion | flops 3759931392 | bytes 12058624 | tf_op jit(solution)/shard_map/dot_general | solution.py:192
  377.5 8.6 %convolution_convert_fusion.1 = bf16[3584,512]{1,0:T(8,128)(2,1)} fusion(bf16[1024,3584]{1,0:T(8,128)(2,1)} %constant_dynamic-update-slice_fusion.32, bf16[1024,1024]{1,0:T(8,128)(2,1)S(1)} %pad_maximum_fusion.2), kind=kOutput, calls=%fused_computation.10 | convolution fusion | flops 3759931392 | bytes 12058624 | tf_op jit(solution)/shard_map/dot_general | solution.py:192
  396.6 13.0 %collective-permute-done.18 = bf16[2,64,3584]{2,1,0:T(8,128)(2,1)S(1)} collective-permute-done((bf16[2,64,3584]{2,1,0:T(8,128)(2,1)}, bf16[2,64,3584]{2,1,0:T(8,128)(2,1)S(1)}, u32[]{:S(2)}, u32[]{:S(2)}) %collective-permute-start.18) | collective-permute-done | bytes 917536 | tf_op jit(solution)/shard_map/ppermute | solution.py:125
  411.7 23.6 %collective-permute-done.14 = bf16[2,64,3584]{2,1,0:T(8,128)(2,1)S(1)} collective-permute-done((bf16[2,64,3584]{2,1,0:T(8,128)(2,1)}, bf16[2,64,3584]{2,1,0:T(8,128)(2,1)S(1)}, u32[]{:S(2)}, u32[]{:S(2)}) %collective-permute-start.14) | collective-permute-done | bytes 917536 | tf_op jit(solution)/shard_map/ppermute | solution.py:125
  438.6 8.5 %collective-permute-done.43 = bf16[64,3584]{1,0:T(8,128)(2,1)S(1)} collective-permute-done((bf16[64,3584]{1,0:T(8,128)(2,1)S(1)}, bf16[64,3584]{1,0:T(8,128)(2,1)S(1)}, u32[]{:S(2)}, u32[]{:S(2)}) %collective-permute-start.43) | collective-permute-done | bytes 458784 | tf_op jit(solution)/shard_map/ppermute | solution.py:125
  451.5 16.5 %collective-permute-done.55 = bf16[64,3584]{1,0:T(8,128)(2,1)S(1)} collective-permute-done((bf16[64,3584]{1,0:T(8,128)(2,1)S(1)}, bf16[64,3584]{1,0:T(8,128)(2,1)S(1)}, u32[]{:S(2)}, u32[]{:S(2)}) %collective-permute-start.55) | collective-permute-done | bytes 458784 | tf_op jit(solution)/shard_map/ppermute | solution.py:129
  471.4 3.3 collective-permute-start.47
  474.7 7.2 %collective-permute-done.27 = bf16[64,3584]{1,0:T(8,128)(2,1)S(1)} collective-permute-done((bf16[64,3584]{1,0:T(8,128)(2,1)S(1)}, bf16[64,3584]{1,0:T(8,128)(2,1)S(1)}, u32[]{:S(2)}, u32[]{:S(2)}) %collective-permute-start.27) | collective-permute-done | bytes 458784 | tf_op jit(solution)/shard_map/ppermute | solution.py:129
  483.2 4.6 collective-permute-start.56
  488.1 2.9 collective-permute-start.19
  493.6 3.9 collective-permute-done.56
  497.5 2.2 collective-permute-start.28
  501.1 3.3 collective-permute-start.33
  504.4 3.7 collective-permute-start.54
  508.1 2.2 collective-permute-start.57
  512.5 2.3 collective-permute-done.54
  514.8 3.7 collective-permute-start.26
  518.4 2.2 collective-permute-start.29
  522.7 2.4 collective-permute-done.26
  525.1 3.7 collective-permute-done.29
  530.9 9.4 %fusion = bf16[1,3584,512]{2,1,0:T(8,128)(2,1)} fusion(bf16[3584,512]{1,0:T(8,128)(2,1)} %collective-permute-done.73, bf16[1024,3584]{1,0:T(8,128)(2,1)} %constant_dynamic-update-slice_fusion.32, bf16[1024,1024]{1,0:T(8,128)(2,1)S(1)} %pad_maximum_fusion.2), kind=kOutput, calls=%fused_computation.11 | convolution fusion | flops 3763601408 | bytes 15728640 | tf_op jit(solution)/shard_map/dot_general | solution.py:192
  540.4 5.7 %fusion.1 = bf16[1,512,3584]{2,1,0:T(8,128)(2,1)} fusion(bf16[512,3584]{1,0:T(8,128)(2,1)S(1)} %collective-permute-done.74, bf16[1024,3584]{1,0:T(8,128)(2,1)S(1)} %bitcast.260, bf16[1024,1024]{1,0:T(8,128)(2,1)S(1)} %pad_maximum_fusion.3), kind=kOutput, calls=%fused_computation.12 | convolution fusion | flops 3763601408 | bytes 15728640 | tf_op jit(solution)/shard_map/dot_general | solution.py:192
  (355 shorter events, 126.6 us)
Async XLA Ops:
  0.6 61.1 %collective-permute-start.6 = (bf16[64,3584]{1,0:T(8,128)(2,1)}, bf16[64,3584]{1,0:T(8,128)(2,1)S(1)}, u32[]{:S(2)}, u32[]{:S(2)}) collective-permute-start(bf16[64,3584]{1,0:T(8,128)(2,1)} %param.6), channel_id=1, source_target_pairs={{24,16},{26,18},{28,20},{30,22},{16,8},{18,10},{20,12},{22,14},{8,... | collective-permute-start | bytes 1376264 | tf_op jit(solution)/shard_map/ppermute | solution.py:129
  3.1 12.3 %collective-permute-start = (bf16[64,3584]{1,0:T(8,128)(2,1)}, bf16[64,3584]{1,0:T(8,128)(2,1)S(1)}, u32[]{:S(2)}, u32[]{:S(2)}) collective-permute-start(bf16[64,3584]{1,0:T(8,128)(2,1)} %param.6), channel_id=1, source_target_pairs={{0,2},{2,0},{4,6},{6,4},{8,10},{10,8},{12,14},{14,12},{16,18},{18,... | collective-permute-start | bytes 1376264 | tf_op jit(solution)/shard_map/ppermute | solution.py:125
  4.7 57.7 %collective-permute-start.9 = (bf16[64,3584]{1,0:T(8,128)(2,1)}, bf16[64,3584]{1,0:T(8,128)(2,1)S(1)}, u32[]{:S(2)}, u32[]{:S(2)}) collective-permute-start(bf16[64,3584]{1,0:T(8,128)(2,1)} %param.6), channel_id=1, source_target_pairs={{0,8},{2,10},{4,12},{6,14},{8,16},{10,18},{12,20},{14,22},{16,24},... | collective-permute-start | bytes 1376264 | tf_op jit(solution)/shard_map/ppermute | solution.py:129
  8.2 57.5 %collective-permute-start.34 = (bf16[64,3584]{1,0:T(8,128)(2,1)}, bf16[64,3584]{1,0:T(8,128)(2,1)S(1)}, u32[]{:S(2)}, u32[]{:S(2)}) collective-permute-start(bf16[64,3584]{1,0:T(8,128)(2,1)} %param.9), channel_id=1, source_target_pairs={{24,16},{26,18},{28,20},{30,22},{16,8},{18,10},{20,12},{22,14},{8,... | collective-permute-start | bytes 1376264 | tf_op jit(solution)/shard_map/ppermute | solution.py:129
  10.5 13.7 %collective-permute-start.30 = (bf16[64,3584]{1,0:T(8,128)(2,1)}, bf16[64,3584]{1,0:T(8,128)(2,1)S(1)}, u32[]{:S(2)}, u32[]{:S(2)}) collective-permute-start(bf16[64,3584]{1,0:T(8,128)(2,1)} %param.9), channel_id=1, source_target_pairs={{0,4},{2,6},{4,0},{6,2},{8,12},{10,14},{12,8},{14,10},{16,20},{18,... | collective-permute-start | bytes 1376264 | tf_op jit(solution)/shard_map/ppermute | solution.py:125
  16.5 25.1 %collective-permute-start.1 = (bf16[2,64,3584]{2,1,0:T(8,128)(2,1)S(1)}, bf16[2,64,3584]{2,1,0:T(8,128)(2,1)S(1)}, u32[]{:S(2)}, u32[]{:S(2)}) collective-permute-start(bf16[2,64,3584]{2,1,0:T(8,128)(2,1)S(1)} %pad_maximum_fusion.4), channel_id=1, source_target_pairs={{0,4},{2,6},{4,0},{6,2},{8,12},{10,14},{12,8},{14,10},{16,20},{18,... | collective-permute-start | bytes 2752520 | tf_op jit(solution)/shard_map/ppermute | solution.py:125
  24.3 42.0 %collective-permute-start.37 = (bf16[64,3584]{1,0:T(8,128)(2,1)S(1)}, bf16[64,3584]{1,0:T(8,128)(2,1)S(1)}, u32[]{:S(2)}, u32[]{:S(2)}) collective-permute-start(bf16[64,3584]{1,0:T(8,128)(2,1)S(1)} %copy-done.2), channel_id=1, source_target_pairs={{0,8},{2,10},{4,12},{6,14},{8,16},{10,18},{12,20},{14,22},{16,24},... | collective-permute-start | bytes 1376264 | tf_op jit(solution)/shard_map/ppermute | solution.py:129
  41.6 20.0 %collective-permute-start.31 = (bf16[2,64,3584]{2,1,0:T(8,128)(2,1)S(1)}, bf16[2,64,3584]{2,1,0:T(8,128)(2,1)S(1)}, u32[]{:S(2)}, u32[]{:S(2)}) collective-permute-start(bf16[2,64,3584]{2,1,0:T(8,128)(2,1)S(1)} %pad_maximum_fusion.12), channel_id=1, source_target_pairs={{0,2},{2,0},{4,6},{6,4},{8,10},{10,8},{12,14},{14,12},{16,18},{18,... | collective-permute-start | bytes 2752520 | tf_op jit(solution)/shard_map/ppermute | solution.py:125
  61.7 93.2 %collective-permute-start.2 = (bf16[3584,512]{1,0:T(8,128)(2,1)S(1)}, bf16[3584,512]{1,0:T(8,128)(2,1)S(1)}, u32[]{:S(2)}, u32[]{:S(2)}) collective-permute-start(bf16[3584,512]{1,0:T(8,128)(2,1)S(1)} %bitcast.284), channel_id=1, source_target_pairs={{0,1},{1,0},{2,3},{3,2},{4,5},{5,4},{6,7},{7,6},{8,9},{9,8},{10,11... | collective-permute-start | bytes 11010056 | tf_op jit(solution)/shard_map/ppermute | solution.py:220
  61.8 101.0 %collective-permute-start.3 = (bf16[512,3584]{1,0:T(8,128)(2,1)S(1)}, bf16[512,3584]{1,0:T(8,128)(2,1)S(1)}, u32[]{:S(2)}, u32[]{:S(2)}) collective-permute-start(bf16[512,3584]{1,0:T(8,128)(2,1)S(1)} %bitcast.294), channel_id=1, source_target_pairs={{0,1},{1,0},{2,3},{3,2},{4,5},{5,4},{6,7},{7,6},{8,9},{9,8},{10,11... | collective-permute-start | bytes 11010056 | tf_op jit(solution)/shard_map/ppermute | solution.py:221
  62.4 60.2 %collective-permute-start.7 = (bf16[64,3584]{1,0:T(8,128)(2,1)S(1)}, bf16[64,3584]{1,0:T(8,128)(2,1)}, u32[]{:S(2)}, u32[]{:S(2)}) collective-permute-start(bf16[64,3584]{1,0:T(8,128)(2,1)S(1)} %collective-permute-done.6), channel_id=1, source_target_pairs={{16,8},{18,10},{20,12},{22,14},{8,0},{10,2},{12,4},{14,6},{17,9},{... | collective-permute-start | bytes 1376264 | tf_op jit(solution)/shard_map/ppermute | solution.py:129
  65.7 12.3 %collective-permute-start.16 = (bf16[64,3584]{1,0:T(8,128)(2,1)S(1)}, bf16[64,3584]{1,0:T(8,128)(2,1)S(1)}, u32[]{:S(2)}, u32[]{:S(2)}) collective-permute-start(bf16[64,3584]{1,0:T(8,128)(2,1)S(1)} %get-tuple-element.18), channel_id=1, source_target_pairs={{0,2},{2,0},{4,6},{6,4},{8,10},{10,8},{12,14},{14,12},{16,18},{18,... | collective-permute-start | bytes 1376264 | tf_op jit(solution)/shard_map/ppermute | solution.py:125
  66.4 12.2 %collective-permute-start.44 = (bf16[64,3584]{1,0:T(8,128)(2,1)S(1)}, bf16[64,3584]{1,0:T(8,128)(2,1)S(1)}, u32[]{:S(2)}, u32[]{:S(2)}) collective-permute-start(bf16[64,3584]{1,0:T(8,128)(2,1)S(1)} %get-tuple-element.12), channel_id=1, source_target_pairs={{0,4},{2,6},{4,0},{6,2},{8,12},{10,14},{12,8},{14,10},{16,20},{18,... | collective-permute-start | bytes 1376264 | tf_op jit(solution)/shard_map/ppermute | solution.py:125
  78.1 21.2 %collective-permute-start.17 = (bf16[2,64,3584]{2,1,0:T(8,128)(2,1)S(1)}, bf16[2,64,3584]{2,1,0:T(8,128)(2,1)S(1)}, u32[]{:S(2)}, u32[]{:S(2)}) collective-permute-start(bf16[2,64,3584]{2,1,0:T(8,128)(2,1)S(1)} %pad_maximum_fusion.8), channel_id=1, source_target_pairs={{0,4},{2,6},{4,0},{6,2},{8,12},{10,14},{12,8},{14,10},{16,20},{18,... | collective-permute-start | bytes 2752520 | tf_op jit(solution)/shard_map/ppermute | solution.py:125
  78.7 45.8 %collective-permute-start.10 = (bf16[64,3584]{1,0:T(8,128)(2,1)S(1)}, bf16[64,3584]{1,0:T(8,128)(2,1)}, u32[]{:S(2)}, u32[]{:S(2)}) collective-permute-start(bf16[64,3584]{1,0:T(8,128)(2,1)S(1)} %collective-permute-done.9), channel_id=1, source_target_pairs={{8,16},{10,18},{12,20},{14,22},{16,24},{18,26},{20,28},{22,30},{9,... | collective-permute-start | bytes 1376264 | tf_op jit(solution)/shard_map/ppermute | solution.py:129
  99.3 20.2 %collective-permute-start.45 = (bf16[2,64,3584]{2,1,0:T(8,128)(2,1)S(1)}, bf16[2,64,3584]{2,1,0:T(8,128)(2,1)S(1)}, u32[]{:S(2)}, u32[]{:S(2)}) collective-permute-start(bf16[2,64,3584]{2,1,0:T(8,128)(2,1)S(1)} %pad_maximum_fusion.16), channel_id=1, source_target_pairs={{0,2},{2,0},{4,6},{6,4},{8,10},{10,8},{12,14},{14,12},{16,18},{18,... | collective-permute-start | bytes 2752520 | tf_op jit(solution)/shard_map/ppermute | solution.py:125
  119.5 9.6 %collective-permute-start.35 = (bf16[64,3584]{1,0:T(8,128)(2,1)S(1)}, bf16[64,3584]{1,0:T(8,128)(2,1)}, u32[]{:S(2)}, u32[]{:S(2)}) collective-permute-start(bf16[64,3584]{1,0:T(8,128)(2,1)S(1)} %collective-permute-done.34), channel_id=1, source_target_pairs={{16,8},{18,10},{20,12},{22,14},{8,0},{10,2},{12,4},{14,6},{17,9},{... | collective-permute-start | bytes 1376264 | tf_op jit(solution)/shard_map/ppermute | solution.py:129
  122.6 12.9 %collective-permute-start.38 = (bf16[64,3584]{1,0:T(8,128)(2,1)S(1)}, bf16[64,3584]{1,0:T(8,128)(2,1)}, u32[]{:S(2)}, u32[]{:S(2)}) collective-permute-start(bf16[64,3584]{1,0:T(8,128)(2,1)S(1)} %collective-permute-done.37), channel_id=1, source_target_pairs={{8,16},{10,18},{12,20},{14,22},{16,24},{18,26},{20,28},{22,30},{9,... | collective-permute-start | bytes 1376264 | tf_op jit(solution)/shard_map/ppermute | solution.py:129
  124.5 56.5 %collective-permute-start.8 = (bf16[64,3584]{1,0:T(8,128)(2,1)}, bf16[64,3584]{1,0:T(8,128)(2,1)}, u32[]{:S(2)}, u32[]{:S(2)}) collective-permute-start(bf16[64,3584]{1,0:T(8,128)(2,1)} %collective-permute-done.7), channel_id=1, source_target_pairs={{8,0},{10,2},{12,4},{14,6},{9,1},{11,3},{13,5},{15,7}} | collective-permute-start | bytes 1376264 | tf_op jit(solution)/shard_map/ppermute | solution.py:129
  129.1 51.9 %collective-permute-start.11 = (bf16[64,3584]{1,0:T(8,128)(2,1)}, bf16[64,3584]{1,0:T(8,128)(2,1)}, u32[]{:S(2)}, u32[]{:S(2)}) collective-permute-start(bf16[64,3584]{1,0:T(8,128)(2,1)} %collective-permute-done.10), channel_id=1, source_target_pairs={{16,24},{18,26},{20,28},{22,30},{17,25},{19,27},{21,29},{23,31}} | collective-permute-start | bytes 1376264 | tf_op jit(solution)/shard_map/ppermute | solution.py:129
  135.5 8.5 %collective-permute-start.20 = (bf16[64,3584]{1,0:T(8,128)(2,1)S(1)}, bf16[64,3584]{1,0:T(8,128)(2,1)S(1)}, u32[]{:S(2)}, u32[]{:S(2)}) collective-permute-start(bf16[64,3584]{1,0:T(8,128)(2,1)S(1)} %get-tuple-element.16), channel_id=1, source_target_pairs={{0,2},{2,0},{4,6},{6,4},{8,10},{10,8},{12,14},{14,12},{16,18},{18,... | collective-permute-start | bytes 1376264 | tf_op jit(solution)/shard_map/ppermute | solution.py:125
  143.9 8.5 %collective-permute-start.48 = (bf16[64,3584]{1,0:T(8,128)(2,1)S(1)}, bf16[64,3584]{1,0:T(8,128)(2,1)S(1)}, u32[]{:S(2)}, u32[]{:S(2)}) collective-permute-start(bf16[64,3584]{1,0:T(8,128)(2,1)S(1)} %get-tuple-element.10), channel_id=1, source_target_pairs={{0,4},{2,6},{4,0},{6,2},{8,12},{10,14},{12,8},{14,10},{16,20},{18,... | collective-permute-start | bytes 1376264 | tf_op jit(solution)/shard_map/ppermute | solution.py:125
  152.4 46.9 %collective-permute-start.36 = (bf16[64,3584]{1,0:T(8,128)(2,1)}, bf16[64,3584]{1,0:T(8,128)(2,1)}, u32[]{:S(2)}, u32[]{:S(2)}) collective-permute-start(bf16[64,3584]{1,0:T(8,128)(2,1)} %collective-permute-done.35), channel_id=1, source_target_pairs={{8,0},{10,2},{12,4},{14,6},{9,1},{11,3},{13,5},{15,7}} | collective-permute-start | bytes 1376264 | tf_op jit(solution)/shard_map/ppermute | solution.py:129
  154.9 44.5 %collective-permute-start.39 = (bf16[64,3584]{1,0:T(8,128)(2,1)}, bf16[64,3584]{1,0:T(8,128)(2,1)}, u32[]{:S(2)}, u32[]{:S(2)}) collective-permute-start(bf16[64,3584]{1,0:T(8,128)(2,1)} %collective-permute-done.38), channel_id=1, source_target_pairs={{16,24},{18,26},{20,28},{22,30},{17,25},{19,27},{21,29},{23,31}} | collective-permute-start | bytes 1376264 | tf_op jit(solution)/shard_map/ppermute | solution.py:129
  162.8 15.8 %collective-permute-start.21 = (bf16[2,64,3584]{2,1,0:T(8,128)(2,1)}, bf16[2,64,3584]{2,1,0:T(8,128)(2,1)S(1)}, u32[]{:S(2)}, u32[]{:S(2)}) collective-permute-start(bf16[2,64,3584]{2,1,0:T(8,128)(2,1)} %pad_maximum_fusion.10), channel_id=1, source_target_pairs={{0,4},{2,6},{4,0},{6,2},{8,12},{10,14},{12,8},{14,10},{16,20},{18,... | collective-permute-start | bytes 2752520 | tf_op jit(solution)/shard_map/ppermute | solution.py:125
  178.7 18.2 %collective-permute-start.49 = (bf16[2,64,3584]{2,1,0:T(8,128)(2,1)}, bf16[2,64,3584]{2,1,0:T(8,128)(2,1)S(1)}, u32[]{:S(2)}, u32[]{:S(2)}) collective-permute-start(bf16[2,64,3584]{2,1,0:T(8,128)(2,1)} %pad_maximum_fusion.18), channel_id=1, source_target_pairs={{0,2},{2,0},{4,6},{6,4},{8,10},{10,8},{12,14},{14,12},{16,18},{18,... | collective-permute-start | bytes 2752520 | tf_op jit(solution)/shard_map/ppermute | solution.py:125
  183.1 21.3 %collective-permute-start.12 = (bf16[64,3584]{1,0:T(8,128)(2,1)S(1)}, bf16[64,3584]{1,0:T(8,128)(2,1)S(1)}, u32[]{:S(2)}, u32[]{:S(2)}) collective-permute-start(bf16[64,3584]{1,0:T(8,128)(2,1)S(1)} %get-tuple-element.14), channel_id=1, source_target_pairs={{0,2},{2,0},{4,6},{6,4},{8,10},{10,8},{12,14},{14,12},{16,18},{18,... | collective-permute-start | bytes 1376264 | tf_op jit(solution)/shard_map/ppermute | solution.py:125
  200.6 9.7 %collective-permute-start.40 = (bf16[64,3584]{1,0:T(8,128)(2,1)}, bf16[64,3584]{1,0:T(8,128)(2,1)S(1)}, u32[]{:S(2)}, u32[]{:S(2)}) collective-permute-start(bf16[64,3584]{1,0:T(8,128)(2,1)} %get-tuple-element.8), channel_id=1, source_target_pairs={{0,4},{2,6},{4,0},{6,2},{8,12},{10,14},{12,8},{14,10},{16,20},{18,... | collective-permute-start | bytes 1376264 | tf_op jit(solution)/shard_map/ppermute | solution.py:125
  205.4 14.7 %collective-permute-start.13 = (bf16[2,64,3584]{2,1,0:T(8,128)(2,1)}, bf16[2,64,3584]{2,1,0:T(8,128)(2,1)S(1)}, u32[]{:S(2)}, u32[]{:S(2)}) collective-permute-start(bf16[2,64,3584]{2,1,0:T(8,128)(2,1)} %pad_maximum_fusion.6), channel_id=1, source_target_pairs={{0,4},{2,6},{4,0},{6,2},{8,12},{10,14},{12,8},{14,10},{16,20},{18,... | collective-permute-start | bytes 2752520 | tf_op jit(solution)/shard_map/ppermute | solution.py:125
  211.7 13.5 %collective-permute-start.41 = (bf16[2,64,3584]{2,1,0:T(8,128)(2,1)S(1)}, bf16[2,64,3584]{2,1,0:T(8,128)(2,1)S(1)}, u32[]{:S(2)}, u32[]{:S(2)}) collective-permute-start(bf16[2,64,3584]{2,1,0:T(8,128)(2,1)S(1)} %pad_maximum_fusion.14), channel_id=1, source_target_pairs={{0,2},{2,0},{4,6},{6,4},{8,10},{10,8},{12,14},{14,12},{16,18},{18,... | collective-permute-start | bytes 2752520 | tf_op jit(solution)/shard_map/ppermute | solution.py:125
  250.5 5.5 collective-permute-start.68
  261.4 5.4 collective-permute-start.70
  266.8 5.4 collective-permute-start.71
  268.5 5.5 %collective-permute-start.65 = (f32[16,64]{1,0:T(8,128)S(1)}, f32[16,64]{1,0:T(8,128)S(1)}, u32[]{:S(2)}, u32[]{:S(2)}) collective-permute-start(f32[16,64]{1,0:T(8,128)S(1)} %collective-permute-done.64), channel_id=1, source_target_pairs={{0,2},{2,4},{4,6},{6,8},{8,10},{10,12},{12,14},{14,16},{16,18},{18... | collective-permute-start | bytes 12296 | tf_op jit(solution)/shard_map/ppermute | solution.py:16
  335.2 50.9 %collective-permute-start.32 = (bf16[2,64,3584]{2,1,0:T(8,128)(2,1)S(1)}, bf16[2,64,3584]{2,1,0:T(8,128)(2,1)}, u32[]{:S(2)}, u32[]{:S(2)}) collective-permute-start(bf16[2,64,3584]{2,1,0:T(8,128)(2,1)S(1)} %pad_maximum_fusion.13), channel_id=1, source_target_pairs={{0,2},{2,0},{4,6},{6,4},{8,10},{10,8},{12,14},{14,12},{16,18},{18,... | collective-permute-start | bytes 2752520 | tf_op jit(solution)/shard_map/ppermute | solution.py:125
  341.2 48.0 %collective-permute-start.46 = (bf16[2,64,3584]{2,1,0:T(8,128)(2,1)S(1)}, bf16[2,64,3584]{2,1,0:T(8,128)(2,1)}, u32[]{:S(2)}, u32[]{:S(2)}) collective-permute-start(bf16[2,64,3584]{2,1,0:T(8,128)(2,1)S(1)} %pad_maximum_fusion.17), channel_id=1, source_target_pairs={{0,2},{2,0},{4,6},{6,4},{8,10},{10,8},{12,14},{14,12},{16,18},{18,... | collective-permute-start | bytes 2752520 | tf_op jit(solution)/shard_map/ppermute | solution.py:125
  352.6 37.9 %collective-permute-start.50 = (bf16[2,64,3584]{2,1,0:T(8,128)(2,1)}, bf16[2,64,3584]{2,1,0:T(8,128)(2,1)}, u32[]{:S(2)}, u32[]{:S(2)}) collective-permute-start(bf16[2,64,3584]{2,1,0:T(8,128)(2,1)} %pad_maximum_fusion.19), channel_id=1, source_target_pairs={{0,2},{2,0},{4,6},{6,4},{8,10},{10,8},{12,14},{14,12},{16,18},{18,... | collective-permute-start | bytes 2752520 | tf_op jit(solution)/shard_map/ppermute | solution.py:125
  354.6 39.1 %collective-permute-start.42 = (bf16[2,64,3584]{2,1,0:T(8,128)(2,1)}, bf16[2,64,3584]{2,1,0:T(8,128)(2,1)}, u32[]{:S(2)}, u32[]{:S(2)}) collective-permute-start(bf16[2,64,3584]{2,1,0:T(8,128)(2,1)} %pad_maximum_fusion.15), channel_id=1, source_target_pairs={{0,2},{2,0},{4,6},{6,4},{8,10},{10,8},{12,14},{14,12},{16,18},{18,... | collective-permute-start | bytes 2752520 | tf_op jit(solution)/shard_map/ppermute | solution.py:125
  359.0 35.9 %collective-permute-start.4 = (bf16[2,64,3584]{2,1,0:T(8,128)(2,1)}, bf16[2,64,3584]{2,1,0:T(8,128)(2,1)}, u32[]{:S(2)}, u32[]{:S(2)}) collective-permute-start(bf16[2,64,3584]{2,1,0:T(8,128)(2,1)} %pad_maximum_fusion.5), channel_id=1, source_target_pairs={{0,4},{2,6},{4,0},{6,2},{8,12},{10,14},{12,8},{14,10},{16,20},{18,... | collective-permute-start | bytes 2752520 | tf_op jit(solution)/shard_map/ppermute | solution.py:125
  386.1 23.5 %collective-permute-start.18 = (bf16[2,64,3584]{2,1,0:T(8,128)(2,1)}, bf16[2,64,3584]{2,1,0:T(8,128)(2,1)S(1)}, u32[]{:S(2)}, u32[]{:S(2)}) collective-permute-start(bf16[2,64,3584]{2,1,0:T(8,128)(2,1)} %pad_maximum_fusion.9), channel_id=1, source_target_pairs={{0,4},{2,6},{4,0},{6,2},{8,12},{10,14},{12,8},{14,10},{16,20},{18,... | collective-permute-start | bytes 2752520 | tf_op jit(solution)/shard_map/ppermute | solution.py:125
  389.3 47.9 %collective-permute-start.22 = (bf16[2,64,3584]{2,1,0:T(8,128)(2,1)S(1)}, bf16[2,64,3584]{2,1,0:T(8,128)(2,1)S(1)}, u32[]{:S(2)}, u32[]{:S(2)}) collective-permute-start(bf16[2,64,3584]{2,1,0:T(8,128)(2,1)S(1)} %pad_maximum_fusion.11), channel_id=1, source_target_pairs={{0,4},{2,6},{4,0},{6,2},{8,12},{10,14},{12,8},{14,10},{16,20},{18,... | collective-permute-start | bytes 2752520 | tf_op jit(solution)/shard_map/ppermute | solution.py:125
  390.5 44.8 %collective-permute-start.14 = (bf16[2,64,3584]{2,1,0:T(8,128)(2,1)}, bf16[2,64,3584]{2,1,0:T(8,128)(2,1)S(1)}, u32[]{:S(2)}, u32[]{:S(2)}) collective-permute-start(bf16[2,64,3584]{2,1,0:T(8,128)(2,1)} %pad_maximum_fusion.7), channel_id=1, source_target_pairs={{0,4},{2,6},{4,0},{6,2},{8,12},{10,14},{12,8},{14,10},{16,20},{18,... | collective-permute-start | bytes 2752520 | tf_op jit(solution)/shard_map/ppermute | solution.py:125
  393.7 137.2 %collective-permute-start.73 = (bf16[3584,512]{1,0:T(8,128)(2,1)}, bf16[3584,512]{1,0:T(8,128)(2,1)}, u32[]{:S(2)}, u32[]{:S(2)}) collective-permute-start(bf16[3584,512]{1,0:T(8,128)(2,1)} %convolution_convert_fusion.1), channel_id=1, source_target_pairs={{0,1},{1,0},{2,3},{3,2},{4,5},{5,4},{6,7},{7,6},{8,9},{9,8},{10,11... | collective-permute-start | bytes 11010056 | tf_op jit(solution)/shard_map/ppermute | solution.py:251
  394.9 145.4 %collective-permute-start.74 = (bf16[512,3584]{1,0:T(8,128)(2,1)}, bf16[512,3584]{1,0:T(8,128)(2,1)S(1)}, u32[]{:S(2)}, u32[]{:S(2)}) collective-permute-start(bf16[512,3584]{1,0:T(8,128)(2,1)} %convolution_convert_fusion), channel_id=1, source_target_pairs={{0,1},{1,0},{2,3},{3,2},{4,5},{5,4},{6,7},{7,6},{8,9},{9,8},{10,11... | collective-permute-start | bytes 11010056 | tf_op jit(solution)/shard_map/ppermute | solution.py:250
  409.6 40.9 %collective-permute-start.51 = (bf16[64,3584]{1,0:T(8,128)(2,1)S(1)}, bf16[64,3584]{1,0:T(8,128)(2,1)S(1)}, u32[]{:S(2)}, u32[]{:S(2)}) collective-permute-start(bf16[64,3584]{1,0:T(8,128)(2,1)S(1)} %fusion.102), channel_id=1, source_target_pairs={{0,4},{2,6},{4,0},{6,2},{8,12},{10,14},{12,8},{14,10},{16,20},{18,... | collective-permute-start | bytes 1376264 | tf_op jit(solution)/shard_map/ppermute | solution.py:125
  435.3 11.8 %collective-permute-start.43 = (bf16[64,3584]{1,0:T(8,128)(2,1)S(1)}, bf16[64,3584]{1,0:T(8,128)(2,1)S(1)}, u32[]{:S(2)}, u32[]{:S(2)}) collective-permute-start(bf16[64,3584]{1,0:T(8,128)(2,1)S(1)} %fusion.106), channel_id=1, source_target_pairs={{0,4},{2,6},{4,0},{6,2},{8,12},{10,14},{12,8},{14,10},{16,20},{18,... | collective-permute-start | bytes 1376264 | tf_op jit(solution)/shard_map/ppermute | solution.py:125
  437.1 12.5 %collective-permute-start.15 = (bf16[64,3584]{1,0:T(8,128)(2,1)S(1)}, bf16[64,3584]{1,0:T(8,128)(2,1)S(1)}, u32[]{:S(2)}, u32[]{:S(2)}) collective-permute-start(bf16[64,3584]{1,0:T(8,128)(2,1)S(1)} %fusion.114), channel_id=1, source_target_pairs={{0,2},{2,0},{4,6},{6,4},{8,10},{10,8},{12,14},{14,12},{16,18},{18,... | collective-permute-start | bytes 1376264 | tf_op jit(solution)/shard_map/ppermute | solution.py:125
  448.3 19.7 %collective-permute-start.55 = (bf16[64,3584]{1,0:T(8,128)(2,1)S(1)}, bf16[64,3584]{1,0:T(8,128)(2,1)S(1)}, u32[]{:S(2)}, u32[]{:S(2)}) collective-permute-start(bf16[64,3584]{1,0:T(8,128)(2,1)S(1)} %add_convert_fusion.7), channel_id=1, source_target_pairs={{24,16},{26,18},{28,20},{30,22},{25,17},{27,19},{29,21},{31,23}} | collective-permute-start | bytes 1376264 | tf_op jit(solution)/shard_map/ppermute | solution.py:129
  449.6 19.7 %collective-permute-start.52 = (bf16[64,3584]{1,0:T(8,128)(2,1)S(1)}, bf16[64,3584]{1,0:T(8,128)(2,1)S(1)}, u32[]{:S(2)}, u32[]{:S(2)}) collective-permute-start(bf16[64,3584]{1,0:T(8,128)(2,1)S(1)} %add_convert_fusion.7), channel_id=1, source_target_pairs={{0,8},{2,10},{4,12},{6,14},{1,9},{3,11},{5,13},{7,15}} | collective-permute-start | bytes 1376264 | tf_op jit(solution)/shard_map/ppermute | solution.py:129
  450.5 20.9 %collective-permute-start.23 = (bf16[64,3584]{1,0:T(8,128)(2,1)S(1)}, bf16[64,3584]{1,0:T(8,128)(2,1)S(1)}, u32[]{:S(2)}, u32[]{:S(2)}) collective-permute-start(bf16[64,3584]{1,0:T(8,128)(2,1)S(1)} %fusion.110), channel_id=1, source_target_pairs={{0,2},{2,0},{4,6},{6,4},{8,10},{10,8},{12,14},{14,12},{16,18},{18,... | collective-permute-start | bytes 1376264 | tf_op jit(solution)/shard_map/ppermute | solution.py:125
  468.1 13.9 %collective-permute-start.27 = (bf16[64,3584]{1,0:T(8,128)(2,1)S(1)}, bf16[64,3584]{1,0:T(8,128)(2,1)S(1)}, u32[]{:S(2)}, u32[]{:S(2)}) collective-permute-start(bf16[64,3584]{1,0:T(8,128)(2,1)S(1)} %add_convert_fusion.14), channel_id=1, source_target_pairs={{24,16},{26,18},{28,20},{30,22},{25,17},{27,19},{29,21},{31,23}} | collective-permute-start | bytes 1376264 | tf_op jit(solution)/shard_map/ppermute | solution.py:129
  469.4 13.9 %collective-permute-start.24 = (bf16[64,3584]{1,0:T(8,128)(2,1)S(1)}, bf16[64,3584]{1,0:T(8,128)(2,1)S(1)}, u32[]{:S(2)}, u32[]{:S(2)}) collective-permute-start(bf16[64,3584]{1,0:T(8,128)(2,1)S(1)} %add_convert_fusion.14), channel_id=1, source_target_pairs={{0,8},{2,10},{4,12},{6,14},{1,9},{3,11},{5,13},{7,15}} | collective-permute-start | bytes 1376264 | tf_op jit(solution)/shard_map/ppermute | solution.py:129
  471.4 16.7 %collective-permute-start.47 = (bf16[64,3584]{1,0:T(8,128)(2,1)S(1)}, bf16[64,3584]{1,0:T(8,128)(2,1)S(1)}, u32[]{:S(2)}, u32[]{:S(2)}) collective-permute-start(bf16[64,3584]{1,0:T(8,128)(2,1)S(1)} %fusion.104), channel_id=1, source_target_pairs={{0,4},{2,6},{4,0},{6,2},{8,12},{10,14},{12,8},{14,10},{16,20},{18,... | collective-permute-start | bytes 1376264 | tf_op jit(solution)/shard_map/ppermute | solution.py:125
  481.9 10.4 %collective-permute-start.53 = (bf16[64,3584]{1,0:T(8,128)(2,1)S(1)}, bf16[64,3584]{1,0:T(8,128)(2,1)S(1)}, u32[]{:S(2)}, u32[]{:S(2)}) collective-permute-start(bf16[64,3584]{1,0:T(8,128)(2,1)S(1)} %get-tuple-element.23), channel_id=1, source_target_pairs={{0,8},{2,10},{4,12},{6,14},{8,16},{10,18},{12,20},{14,22},{1,9},{3... | collective-permute-start | bytes 1376264 | tf_op jit(solution)/shard_map/ppermute | solution.py:129
  483.2 14.2 %collective-permute-start.56 = (bf16[64,3584]{1,0:T(8,128)(2,1)S(1)}, bf16[64,3584]{1,0:T(8,128)(2,1)S(1)}, u32[]{:S(2)}, u32[]{:S(2)}) collective-permute-start(bf16[64,3584]{1,0:T(8,128)(2,1)S(1)} %get-tuple-element.24), channel_id=1, source_target_pairs={{24,16},{26,18},{28,20},{30,22},{16,8},{18,10},{20,12},{22,14},{25... | collective-permute-start | bytes 1376264 | tf_op jit(solution)/shard_map/ppermute | solution.py:129
  488.1 13.0 %collective-permute-start.19 = (bf16[64,3584]{1,0:T(8,128)(2,1)S(1)}, bf16[64,3584]{1,0:T(8,128)(2,1)S(1)}, u32[]{:S(2)}, u32[]{:S(2)}) collective-permute-start(bf16[64,3584]{1,0:T(8,128)(2,1)S(1)} %fusion.112), channel_id=1, source_target_pairs={{0,2},{2,0},{4,6},{6,4},{8,10},{10,8},{12,14},{14,12},{16,18},{18,... | collective-permute-start | bytes 1376264 | tf_op jit(solution)/shard_map/ppermute | solution.py:125
  492.3 12.1 %collective-permute-start.25 = (bf16[64,3584]{1,0:T(8,128)(2,1)S(1)}, bf16[64,3584]{1,0:T(8,128)(2,1)S(1)}, u32[]{:S(2)}, u32[]{:S(2)}) collective-permute-start(bf16[64,3584]{1,0:T(8,128)(2,1)S(1)} %get-tuple-element.25), channel_id=1, source_target_pairs={{0,8},{2,10},{4,12},{6,14},{8,16},{10,18},{12,20},{14,22},{1,9},{3... | collective-permute-start | bytes 1376264 | tf_op jit(solution)/shard_map/ppermute | solution.py:129
  497.5 10.6 %collective-permute-start.28 = (bf16[64,3584]{1,0:T(8,128)(2,1)S(1)}, bf16[64,3584]{1,0:T(8,128)(2,1)S(1)}, u32[]{:S(2)}, u32[]{:S(2)}) collective-permute-start(bf16[64,3584]{1,0:T(8,128)(2,1)S(1)} %get-tuple-element.26), channel_id=1, source_target_pairs={{24,16},{26,18},{28,20},{30,22},{16,8},{18,10},{20,12},{22,14},{25... | collective-permute-start | bytes 1376264 | tf_op jit(solution)/shard_map/ppermute | solution.py:129
  501.1 9.8 %collective-permute-start.33 = (bf16[64,3584]{1,0:T(8,128)(2,1)S(1)}, bf16[64,3584]{1,0:T(8,128)(2,1)S(1)}, u32[]{:S(2)}, u32[]{:S(2)}) collective-permute-start(bf16[64,3584]{1,0:T(8,128)(2,1)S(1)} %fusion.108), channel_id=1, source_target_pairs={{0,4},{2,6},{4,0},{6,2},{8,12},{10,14},{12,8},{14,10},{16,20},{18,... | collective-permute-start | bytes 1376264 | tf_op jit(solution)/shard_map/ppermute | solution.py:125
  504.4 10.4 %collective-permute-start.54 = (bf16[64,3584]{1,0:T(8,128)(2,1)S(1)}, bf16[64,3584]{1,0:T(8,128)(2,1)S(1)}, u32[]{:S(2)}, u32[]{:S(2)}) collective-permute-start(bf16[64,3584]{1,0:T(8,128)(2,1)S(1)} %get-tuple-element.19), channel_id=1, source_target_pairs={{0,8},{2,10},{4,12},{6,14},{8,16},{10,18},{12,20},{14,22},{16,24},... | collective-permute-start | bytes 1376264 | tf_op jit(solution)/shard_map/ppermute | solution.py:129
  508.1 10.4 %collective-permute-start.57 = (bf16[64,3584]{1,0:T(8,128)(2,1)S(1)}, bf16[64,3584]{1,0:T(8,128)(2,1)S(1)}, u32[]{:S(2)}, u32[]{:S(2)}) collective-permute-start(bf16[64,3584]{1,0:T(8,128)(2,1)S(1)} %get-tuple-element.20), channel_id=1, source_target_pairs={{24,16},{26,18},{28,20},{30,22},{16,8},{18,10},{20,12},{22,14},{8,... | collective-permute-start | bytes 1376264 | tf_op jit(solution)/shard_map/ppermute | solution.py:129
  510.9 11.8 %collective-permute-start.5 = (bf16[64,3584]{1,0:T(8,128)(2,1)S(1)}, bf16[64,3584]{1,0:T(8,128)(2,1)S(1)}, u32[]{:S(2)}, u32[]{:S(2)}) collective-permute-start(bf16[64,3584]{1,0:T(8,128)(2,1)S(1)} %fusion.116), channel_id=1, source_target_pairs={{0,2},{2,0},{4,6},{6,4},{8,10},{10,8},{12,14},{14,12},{16,18},{18,... | collective-permute-start | bytes 1376264 | tf_op jit(solution)/shard_map/ppermute | solution.py:125
  514.8 10.4 %collective-permute-start.26 = (bf16[64,3584]{1,0:T(8,128)(2,1)S(1)}, bf16[64,3584]{1,0:T(8,128)(2,1)S(1)}, u32[]{:S(2)}, u32[]{:S(2)}) collective-permute-start(bf16[64,3584]{1,0:T(8,128)(2,1)S(1)} %get-tuple-element.21), channel_id=1, source_target_pairs={{0,8},{2,10},{4,12},{6,14},{8,16},{10,18},{12,20},{14,22},{16,24},... | collective-permute-start | bytes 1376264 | tf_op jit(solution)/shard_map/ppermute | solution.py:129
  518.4 10.4 %collective-permute-start.29 = (bf16[64,3584]{1,0:T(8,128)(2,1)S(1)}, bf16[64,3584]{1,0:T(8,128)(2,1)S(1)}, u32[]{:S(2)}, u32[]{:S(2)}) collective-permute-start(bf16[64,3584]{1,0:T(8,128)(2,1)S(1)} %get-tuple-element.22), channel_id=1, source_target_pairs={{24,16},{26,18},{28,20},{30,22},{16,8},{18,10},{20,12},{22,14},{8,... | collective-permute-start | bytes 1376264 | tf_op jit(solution)/shard_map/ppermute | solution.py:129
  (63 other events, 892.4 us)
